TPU v7x, 1024 devices: a whole 8x8x8 slice. The times are simulated.
1024 devices in a mesh: stream: 8 (over y_hi, core), cross: 128 (over x, y_lo, z).
Axes of the slice: x: 8, y: 8 (y_hi: 4, y_lo: 2; y = y_hi * 2 + y_lo), z: 8, core: 2. Of those that a mesh axis runs over, the one named last changes fastest.
Arguments:
- pressure: float32 [192, 1024, 128], P('stream', 'cross'), may hold values from -6 to 6
- geo_diag: float32 [3, 192, 1024, 128], P(None, 'stream', 'cross'), may hold values from 0.004 to 0.04
- geo_off: float32 [3, 192, 1024, 128], P(None, 'stream', 'cross'), may hold values from -0.008 to 0.008
- modes_first: float32 [24, 10, 10], P('stream'), may hold values from -2 to 2
- modes_second: float32 [128, 10, 10], P('cross'), may hold values from -2 to 2
- modes_third: float32 [16, 10, 10], replicated, may hold values from -2 to 2
- eigen_first: float32 [24, 10], P('stream'), may hold values from 0.3 to 3
- eigen_second: float32 [128, 10], P('cross'), may hold values from 0.3 to 3
- eigen_third: float32 [16, 10], replicated, may hold values from 0.3 to 3
Outputs:
- operator_out: float32 [192, 1024, 128], P('stream', 'cross')
- preconditioned: float32 [192, 1024, 128], P('stream', 'cross')
All inputs are finite; a program needn't handle non-finite values.
Results may differ from a plain program's by a relative error of at most 0.00013.
Values sent between devices are 32-bit elements; how exact they have to be, the bound alone decides.
A program may use at most 32 MiB of HBM per device.

v0:
```python
import jax
import jax.numpy as jnp
import numpy as np
from jax import lax
from jax.sharding import PartitionSpec as P

N1 = 8


HIGHEST = lax.Precision.HIGHEST


def padded_2(cells, sides, width):
    for axis, dim in sides:
        count = lax.axis_size(axis)
        ends = count - 1
        head = lax.slice_in_dim(cells, 0, width, axis=dim)
        tail = lax.slice_in_dim(cells, cells.shape[dim] - width, cells.shape[dim], axis=dim)
        cells = jnp.concatenate(
            [
                lax.ppermute(tail, axis, [(i, (i + 1) % count) for i in range(ends)]),
                cells,
                lax.ppermute(head, axis, [((i + 1) % count, i) for i in range(ends)]),
            ],
            axis=dim,
        )
    return cells


def legendre_values(nodes, degree):
    table = np.zeros((nodes.shape[0], degree + 1))
    table[:, 0] = 1.0
    table[:, 1] = nodes
    for order in range(2, degree + 1):
        table[:, order] = (
            (2 * order - 1) * nodes * table[:, order - 1] - (order - 1) * table[:, order - 2]
        ) / order
    return table


def derivative_table(points):
    degree = points - 1
    nodes = np.cos(np.pi * np.arange(points) / degree)
    for sweep in range(100):
        table = legendre_values(nodes, degree)
        nodes = nodes - (nodes * table[:, degree] - table[:, degree - 1]) / (
            points * table[:, degree]
        )
    gll_nodes = nodes[::-1]
    legendre_at = legendre_values(gll_nodes, degree)[:, degree]
    diff_table = np.zeros((points, points))
    for first_index in range(points):
        for second_index in range(points):
            if first_index != second_index:
                diff_table[first_index, second_index] = legendre_at[first_index] / (
                    legendre_at[second_index] * (gll_nodes[first_index] - gll_nodes[second_index])
                )
    diff_table[0, 0] = -degree * (degree + 1) / 4.0
    diff_table[degree, degree] = degree * (degree + 1) / 4.0
    return diff_table


def group_size():
    return 16


def along_first(source, matrix):
    nodes_count = matrix.shape[0]
    blocks = source.shape[0] // nodes_count
    shaped = source.reshape(blocks, nodes_count, source.shape[1], source.shape[2])
    result = jnp.einsum("ij,ajyz->aiyz", matrix, shaped, precision=HIGHEST)
    return result.reshape(source.shape)


def along_second(source, matrix):
    nodes_count = matrix.shape[0]
    blocks = source.shape[1] // nodes_count
    shaped = source.reshape(source.shape[0], blocks, nodes_count, source.shape[2])
    result = jnp.einsum("ij,xbjz->xbiz", matrix, shaped, precision=HIGHEST)
    return result.reshape(source.shape)


def along_third(source, matrix):
    nodes_count = matrix.shape[0]
    blocks = source.shape[2] // nodes_count
    grouped = group_size()
    kron_matrix = jnp.kron(jnp.eye(grouped, dtype=jnp.float32), matrix)
    shaped = source.reshape(
        source.shape[0], source.shape[1], blocks // grouped, grouped * nodes_count
    )
    result = jnp.einsum("xybl,kl->xybk", shaped, kron_matrix, precision=HIGHEST)
    return result.reshape(source.shape)


def modal_first(source, modes, backward):
    blocks = modes.shape[0]
    extent = modes.shape[1]
    shaped = source.reshape(blocks, extent, source.shape[1], source.shape[2])
    if backward:
        result = jnp.einsum("amp,apyz->amyz", modes, shaped, precision=HIGHEST)
    else:
        result = jnp.einsum("amp,amyz->apyz", modes, shaped, precision=HIGHEST)
    return result.reshape(source.shape)


def modal_second(source, modes, backward):
    blocks = modes.shape[0]
    extent = modes.shape[1]
    shaped = source.reshape(source.shape[0], blocks, extent, source.shape[2])
    if backward:
        result = jnp.einsum("bmp,xbpz->xbmz", modes, shaped, precision=HIGHEST)
    else:
        result = jnp.einsum("bmp,xbmz->xbpz", modes, shaped, precision=HIGHEST)
    return result.reshape(source.shape)


def modal_third(source, modes, backward):
    blocks = modes.shape[0]
    extent = modes.shape[1]
    grouped = group_size()
    identity = jnp.eye(grouped, dtype=jnp.float32)
    kron_modes = jnp.einsum(
        "gh,bgmp->bgmhp",
        identity,
        modes.reshape(blocks // grouped, grouped, extent, extent),
        precision=HIGHEST,
    ).reshape(blocks // grouped, grouped * extent, grouped * extent)
    shaped = source.reshape(source.shape[0], source.shape[1], blocks // grouped, grouped * extent)
    if backward:
        result = jnp.einsum("xybp,bmp->xybm", shaped, kron_modes, precision=HIGHEST)
    else:
        result = jnp.einsum("xybm,bmp->xybp", shaped, kron_modes, precision=HIGHEST)
    return result.reshape(source.shape)


def local_laplacian(pressure, geo_diag, geo_off, diff_matrix):
    grad_first = along_first(pressure, diff_matrix)
    grad_second = along_second(pressure, diff_matrix)
    grad_third = along_third(pressure, diff_matrix)
    flux_first = geo_diag[0] * grad_first + geo_off[0] * grad_second + geo_off[1] * grad_third
    flux_second = geo_off[0] * grad_first + geo_diag[1] * grad_second + geo_off[2] * grad_third
    flux_third = geo_off[1] * grad_first + geo_off[2] * grad_second + geo_diag[2] * grad_third
    transposed = diff_matrix.T
    return (
        along_first(flux_first, transposed)
        + along_second(flux_second, transposed)
        + along_third(flux_third, transposed)
    )


def owner_sum_axis(source, dimension, offset, nodes_count):
    length = source.shape[dimension]
    broadcast_shape = [1] * source.ndim
    broadcast_shape[dimension] = length
    local_node = ((jnp.arange(length, dtype=jnp.int32) - offset) % nodes_count).reshape(
        broadcast_shape
    )
    zero_slab = jnp.zeros_like(lax.slice_in_dim(source, 0, 1, axis=dimension))
    previous = jnp.concatenate(
        [zero_slab, lax.slice_in_dim(source, 0, length - 1, axis=dimension)], axis=dimension
    )
    following = jnp.concatenate(
        [lax.slice_in_dim(source, 1, length, axis=dimension), zero_slab], axis=dimension
    )
    return (
        source
        + jnp.where(local_node == 0, previous, 0.0)
        + jnp.where(local_node == nodes_count - 1, following, 0.0)
    )


def owner_sum(source, offset, nodes_count):
    summed = owner_sum_axis(source, 0, offset, nodes_count)
    summed = owner_sum_axis(summed, 1, offset, nodes_count)
    return owner_sum_axis(summed, 2, 0, nodes_count)


def with_blocks(section, dimension, blocks, extent):
    new_shape = list(section.shape)
    new_shape[dimension : dimension + 1] = [blocks, extent]
    return section.reshape(new_shape)


def extend_axis(padded, dimension, blocks, nodes_count):
    extent_all = blocks * nodes_count
    left_part = lax.slice_in_dim(padded, 0, extent_all, stride=nodes_count, axis=dimension)
    middle = lax.slice_in_dim(padded, 2, extent_all + 2, axis=dimension)
    right_part = lax.slice_in_dim(
        padded, nodes_count + 3, extent_all + 4, stride=nodes_count, axis=dimension
    )
    joined = jnp.concatenate(
        [
            with_blocks(left_part, dimension, blocks, 1),
            with_blocks(middle, dimension, blocks, nodes_count),
            with_blocks(right_part, dimension, blocks, 1),
        ],
        axis=dimension + 1,
    )
    new_shape = list(padded.shape)
    new_shape[dimension] = blocks * (nodes_count + 2)
    return joined.reshape(new_shape)


def restrict_axis(source, dimension, blocks, extent):
    shaped = with_blocks(source, dimension, blocks, extent)
    kept_part = lax.slice_in_dim(shaped, 1, extent - 1, axis=dimension + 1)
    new_shape = list(source.shape)
    new_shape[dimension] = blocks * (extent - 2)
    return kept_part.reshape(new_shape)


def fast_solve(
    extended, modes_first, modes_second, modes_third, eigen_first, eigen_second, eigen_third
):
    spectral = modal_first(extended, modes_first, False)
    spectral = modal_second(spectral, modes_second, False)
    spectral = modal_third(spectral, modes_third, False)
    denominator = (
        eigen_first.reshape(-1, 1, 1)
        + eigen_second.reshape(1, -1, 1)
        + eigen_third.reshape(1, 1, -1)
    )
    spectral = spectral / denominator
    solved = modal_first(spectral, modes_first, True)
    solved = modal_second(solved, modes_second, True)
    return modal_third(solved, modes_third, True)


def shards(
    pressure,
    geo_diag,
    geo_off,
    modes_first,
    modes_second,
    modes_third,
    eigen_first,
    eigen_second,
    eigen_third,
):
    nodes_count = N1
    diff_matrix = jnp.asarray(derivative_table(nodes_count), dtype=jnp.float32)
    first_blocks = pressure.shape[0] // nodes_count
    second_blocks = pressure.shape[1] // nodes_count
    third_blocks = pressure.shape[2] // nodes_count
    local_product = local_laplacian(pressure, geo_diag, geo_off, diff_matrix)
    padded = padded_2(local_product, (("stream", 0), ("cross", 1)), 1)
    operator_out = owner_sum(padded, 1, nodes_count)[1:-1, 1:-1]
    rimmed = padded_2(operator_out, (("stream", 0), ("cross", 1)), 2)
    rimmed = jnp.pad(rimmed, ((0, 0), (0, 0), (2, 2)))
    extended = extend_axis(rimmed, 0, first_blocks, nodes_count)
    extended = extend_axis(extended, 1, second_blocks, nodes_count)
    extended = extend_axis(extended, 2, third_blocks, nodes_count)
    solved = fast_solve(
        extended, modes_first, modes_second, modes_third, eigen_first, eigen_second, eigen_third
    )
    restricted = restrict_axis(solved, 0, first_blocks, nodes_count + 2)
    restricted = restrict_axis(restricted, 1, second_blocks, nodes_count + 2)
    restricted = restrict_axis(restricted, 2, third_blocks, nodes_count + 2)
    padded_again = padded_2(restricted, (("stream", 0), ("cross", 1)), 1)
    preconditioned = owner_sum(padded_again, 1, nodes_count)[1:-1, 1:-1]
    return (operator_out, preconditioned)


def solution(mesh):
    in_specs = (
        P("stream", "cross", None),
        P(None, "stream", "cross", None),
        P(None, "stream", "cross", None),
        P("stream", None, None),
        P("cross", None, None),
        P(),
        P("stream", None),
        P("cross", None),
        P(),
    )
    out_specs = (P("stream", "cross", None), P("stream", "cross", None))
    return jax.shard_map(shards, mesh=mesh, in_specs=in_specs, out_specs=out_specs, check_vma=False)
```

profile of v0, /device:TPU:41, one launch (start us, length us, event | category | flops | bytes accessed | tf_op | source)
XLA Modules:
  0.0 99.2 jit_solution(7567982417071110995)
XLA Ops:
  0.7 0.9 broadcast_multiply_fusion
  4.4 6.2 %collective-permute-start = (f32[1,8,128]{2,1,0:T(8,128)S(1)}, f32[1,8,128]{2,1,0:T(8,128)S(1)}, u32[]{:S(2)}, u32[]{:S(2)}) collective-permute-start(f32[1,8,128]{2,1,0:T(8,128)S(1)} %get-tuple-element.28), channel_id=1, source_target_pairs={{0,128},{128,256},{256,384},{384,512},{512,640},{640,768},{768,896... | collective-permute-start | bytes 12296 | tf_op jit(solution)/shard_map/ppermute | solution.py:21
  10.6 1.9 %collective-permute-start.1 = (f32[1,8,128]{2,1,0:T(8,128)S(1)}, f32[1,8,128]{2,1,0:T(8,128)S(1)}, u32[]{:S(2)}, u32[]{:S(2)}) collective-permute-start(f32[1,8,128]{2,1,0:T(8,128)S(1)} %get-tuple-element.29), channel_id=1, source_target_pairs={{128,0},{256,128},{384,256},{512,384},{640,512},{768,640},{896,768... | collective-permute-start | bytes 12296 | tf_op jit(solution)/shard_map/ppermute | solution.py:23
  12.6 5.0 %collective-permute-done.1 = f32[1,8,128]{2,1,0:T(8,128)S(1)} collective-permute-done((f32[1,8,128]{2,1,0:T(8,128)S(1)}, f32[1,8,128]{2,1,0:T(8,128)S(1)}, u32[]{:S(2)}, u32[]{:S(2)}) %collective-permute-start.1) | collective-permute-done | bytes 4128 | tf_op jit(solution)/shard_map/ppermute | solution.py:23
  17.7 4.9 %collective-permute-start.2 = (f32[26,1,128]{2,1,0:T(1,128)S(1)}, f32[26,1,128]{2,1,0:T(1,128)S(1)}, u32[]{:S(2)}, u32[]{:S(2)}) collective-permute-start(f32[26,1,128]{2,1,0:T(1,128)S(1)} %get-tuple-element.26), channel_id=1, source_target_pairs={{0,1},{1,2},{2,3},{3,4},{4,5},{5,6},{6,7},{7,8},{8,9},{9,10},{10,1... | collective-permute-start | bytes 39944 | tf_op jit(solution)/shard_map/ppermute | solution.py:21
  22.6 14.2 %collective-permute-start.3 = (f32[26,1,128]{2,1,0:T(1,128)S(1)}, f32[26,1,128]{2,1,0:T(1,128)S(1)}, u32[]{:S(2)}, u32[]{:S(2)}) collective-permute-start(f32[26,1,128]{2,1,0:T(1,128)S(1)} %get-tuple-element.27), channel_id=1, source_target_pairs={{1,0},{2,1},{3,2},{4,3},{5,4},{6,5},{7,6},{8,7},{9,8},{10,9},{11,1... | collective-permute-start | bytes 39944 | tf_op jit(solution)/shard_map/ppermute | solution.py:23
  36.9 0.7 collective-permute-done.3
  38.3 2.8 %collective-permute-start.4 = (f32[2,8,128]{2,1,0:T(8,128)S(1)}, f32[2,8,128]{2,1,0:T(8,128)S(1)}, u32[]{:S(2)}, u32[]{:S(2)}) collective-permute-start(f32[2,8,128]{2,1,0:T(8,128)S(1)} %get-tuple-element.14), channel_id=1, source_target_pairs={{0,128},{128,256},{256,384},{384,512},{512,640},{640,768},{768,896... | collective-permute-start | bytes 24584 | tf_op jit(solution)/shard_map/ppermute | solution.py:21
  41.2 1.9 %collective-permute-start.5 = (f32[2,8,128]{2,1,0:T(8,128)S(1)}, f32[2,8,128]{2,1,0:T(8,128)S(1)}, u32[]{:S(2)}, u32[]{:S(2)}) collective-permute-start(f32[2,8,128]{2,1,0:T(8,128)S(1)} %get-tuple-element.15), channel_id=1, source_target_pairs={{128,0},{256,128},{384,256},{512,384},{640,512},{768,640},{896,768... | collective-permute-start | bytes 24584 | tf_op jit(solution)/shard_map/ppermute | solution.py:23
  43.3 4.9 %collective-permute-done.5 = f32[2,8,128]{2,1,0:T(8,128)S(1)} collective-permute-done((f32[2,8,128]{2,1,0:T(8,128)S(1)}, f32[2,8,128]{2,1,0:T(8,128)S(1)}, u32[]{:S(2)}, u32[]{:S(2)}) %collective-permute-start.5) | collective-permute-done | bytes 8224 | tf_op jit(solution)/shard_map/ppermute | solution.py:23
  48.3 1.9 %collective-permute-start.6 = (f32[28,2,128]{2,1,0:T(2,128)S(1)}, f32[28,2,128]{2,1,0:T(2,128)S(1)}, u32[]{:S(2)}, u32[]{:S(2)}) collective-permute-start(f32[28,2,128]{2,1,0:T(2,128)S(1)} %get-tuple-element.22), channel_id=1, source_target_pairs={{0,1},{1,2},{2,3},{3,4},{4,5},{5,6},{6,7},{7,8},{8,9},{9,10},{10,1... | collective-permute-start | bytes 86024 | tf_op jit(solution)/shard_map/ppermute | solution.py:21
  50.2 8.3 %collective-permute-start.7 = (f32[28,2,128]{2,1,0:T(2,128)S(1)}, f32[28,2,128]{2,1,0:T(2,128)S(1)}, u32[]{:S(2)}, u32[]{:S(2)}) collective-permute-start(f32[28,2,128]{2,1,0:T(2,128)S(1)} %get-tuple-element.23), channel_id=1, source_target_pairs={{1,0},{2,1},{3,2},{4,3},{5,4},{6,5},{7,6},{8,7},{9,8},{10,9},{11,1... | collective-permute-start | bytes 86024 | tf_op jit(solution)/shard_map/ppermute | solution.py:23
  61.3 1.3 %slice.174 = f32[30,10,16]{2,1,0:T(8,128)S(1)} slice(f32[30,10,132]{2,1,0:T(8,128)S(1)} %maximum_bitcast_fusion), slice={[0:30:1], [0:10:1], [0:128:8]} | slice | bytes 38400 | tf_op jit(solution)/shard_map/slice | solution.py:186
  62.6 1.4 %slice.176 = f32[30,10,16]{2,1,0:T(8,128)S(1)} slice(f32[30,10,132]{2,1,0:T(8,128)S(1)} %maximum_bitcast_fusion), slice={[0:30:1], [0:10:1], [11:132:8]} | slice | bytes 38400 | tf_op jit(solution)/shard_map/slice | solution.py:188
  64.5 1.4 %pad_maximum_fusion = f32[30,10,16,10]{0,3,2,1:T(8,128)} fusion(f32[30,10,16,1]{0,3,2,1:T(1,128)S(1)} %copy.75, f32[30,10,16,8]{0,3,2,1:T(8,128)S(1)} %bitcast.177, f32[30,10,16,1]{0,3,2,1:T(1,128)S(1)} %copy.74), kind=kLoop, calls=%fused_computation.2 | loop fusion | flops 96000 | bytes 384000 | tf_op jit(solution)/shard_map/concatenate | solution.py:191
  66.0 3.0 %reshape.289 = f32[3,10,10,160]{1,0,3,2:T(4,128)S(1)} reshape(f32[30,10,16,10]{0,3,2,1:T(8,128)} %pad_maximum_fusion) | data formatting | bytes 384000 | tf_op jit(solution)/shard_map/reshape;reshape | solution.py:98
  69.0 4.7 %fusion.2 = f32[3,10,10,160]{3,1,2,0:T(8,128)S(1)} fusion(f32[3,10,10,160]{1,0,3,2:T(4,128)S(1)} %reshape.289, f32[3,10,10,1]{2,0,1,3:T(4,128)} %bitcast.192), kind=kOutput, calls=%fused_computation.4 | convolution fusion | flops 5760000 | bytes 385200 | tf_op jit(solution)/shard_map/amp,amyz->apyz/dot_general | solution.py:102
  78.1 2.2 %collective-permute-start.8 = (f32[1,8,128]{2,1,0:T(8,128)S(1)}, f32[1,8,128]{2,1,0:T(8,128)S(1)}, u32[]{:S(2)}, u32[]{:S(2)}) collective-permute-start(f32[1,8,128]{2,1,0:T(8,128)S(1)} %copy.112), channel_id=1, source_target_pairs={{0,128},{128,256},{256,384},{384,512},{512,640},{640,768},{768,896... | collective-permute-start | bytes 12296 | tf_op jit(solution)/shard_map/ppermute | solution.py:21
  80.4 2.2 %collective-permute-start.9 = (f32[1,8,128]{2,1,0:T(8,128)S(1)}, f32[1,8,128]{2,1,0:T(8,128)S(1)}, u32[]{:S(2)}, u32[]{:S(2)}) collective-permute-start(f32[1,8,128]{2,1,0:T(8,128)S(1)} %copy.115), channel_id=1, source_target_pairs={{128,0},{256,128},{384,256},{512,384},{640,512},{768,640},{896,768... | collective-permute-start | bytes 12296 | tf_op jit(solution)/shard_map/ppermute | solution.py:23
  82.9 4.6 %collective-permute-done.9 = f32[1,8,128]{2,1,0:T(8,128)S(1)} collective-permute-done((f32[1,8,128]{2,1,0:T(8,128)S(1)}, f32[1,8,128]{2,1,0:T(8,128)S(1)}, u32[]{:S(2)}, u32[]{:S(2)}) %collective-permute-start.9) | collective-permute-done | bytes 4128 | tf_op jit(solution)/shard_map/ppermute | solution.py:23
  87.6 1.9 %collective-permute-start.10 = (f32[26,1,128]{2,1,0:T(1,128)S(1)}, f32[26,1,128]{2,1,0:T(1,128)S(1)}, u32[]{:S(2)}, u32[]{:S(2)}) collective-permute-start(f32[26,1,128]{2,1,0:T(1,128)S(1)} %get-tuple-element.24), channel_id=1, source_target_pairs={{0,1},{1,2},{2,3},{3,4},{4,5},{5,6},{6,7},{7,8},{8,9},{9,10},{10,1... | collective-permute-start | bytes 39944 | tf_op jit(solution)/shard_map/ppermute | solution.py:21
  89.6 7.6 %collective-permute-start.11 = (f32[26,1,128]{2,1,0:T(1,128)S(1)}, f32[26,1,128]{2,1,0:T(1,128)S(1)}, u32[]{:S(2)}, u32[]{:S(2)}) collective-permute-start(f32[26,1,128]{2,1,0:T(1,128)S(1)} %get-tuple-element.25), channel_id=1, source_target_pairs={{1,0},{2,1},{3,2},{4,3},{5,4},{6,5},{7,6},{8,7},{9,8},{10,9},{11,1... | collective-permute-start | bytes 39944 | tf_op jit(solution)/shard_map/ppermute | solution.py:23
  97.2 0.8 collective-permute-done.11
  98.5 0.7 fusion.10
  (117 shorter events, 11.9 us)
Async XLA Ops:
  3.3 33.6 %copy-start.4 = (f32[16,10,10]{2,0,1:T(8,128)S(1)}, f32[16,10,10]{2,0,1:T(8,128)}, u32[]{:S(2)}) copy-start(f32[16,10,10]{2,0,1:T(8,128)} %param.15) | copy-start | bytes 19204
  4.4 8.2 %collective-permute-start = (f32[1,8,128]{2,1,0:T(8,128)S(1)}, f32[1,8,128]{2,1,0:T(8,128)S(1)}, u32[]{:S(2)}, u32[]{:S(2)}) collective-permute-start(f32[1,8,128]{2,1,0:T(8,128)S(1)} %get-tuple-element.28), channel_id=1, source_target_pairs={{0,128},{128,256},{256,384},{384,512},{512,640},{640,768},{768,896... | collective-permute-start | bytes 12296 | tf_op jit(solution)/shard_map/ppermute | solution.py:21
  10.6 7.0 %collective-permute-start.1 = (f32[1,8,128]{2,1,0:T(8,128)S(1)}, f32[1,8,128]{2,1,0:T(8,128)S(1)}, u32[]{:S(2)}, u32[]{:S(2)}) collective-permute-start(f32[1,8,128]{2,1,0:T(8,128)S(1)} %get-tuple-element.29), channel_id=1, source_target_pairs={{128,0},{256,128},{384,256},{512,384},{640,512},{768,640},{896,768... | collective-permute-start | bytes 12296 | tf_op jit(solution)/shard_map/ppermute | solution.py:23
  12.5 25.2 %copy-start.16 = (pred[26]{0:T(512)(128)(4,1)}, pred[26]{0:T(512)(128)(4,1)S(1)}, u32[]{:S(2)}) copy-start(pred[26]{0:T(512)(128)(4,1)S(1)} %get-tuple-element.34) | copy-start | bytes 82
  12.6 25.2 %copy-start.18 = (pred[26]{0:T(512)(128)(4,1)}, pred[26]{0:T(512)(128)(4,1)S(1)}, u32[]{:S(2)}) copy-start(pred[26]{0:T(512)(128)(4,1)S(1)} %get-tuple-element.35) | copy-start | bytes 82
  12.6 25.3 %copy-start.12 = (pred[10]{0:T(512)(128)(4,1)}, pred[10]{0:T(512)(128)(4,1)S(1)}, u32[]{:S(2)}) copy-start(pred[10]{0:T(512)(128)(4,1)S(1)} %get-tuple-element.36) | copy-start | bytes 34
  12.6 25.3 %copy-start.14 = (pred[10]{0:T(512)(128)(4,1)}, pred[10]{0:T(512)(128)(4,1)S(1)}, u32[]{:S(2)}) copy-start(pred[10]{0:T(512)(128)(4,1)S(1)} %get-tuple-element.37) | copy-start | bytes 34
  17.7 19.2 %collective-permute-start.2 = (f32[26,1,128]{2,1,0:T(1,128)S(1)}, f32[26,1,128]{2,1,0:T(1,128)S(1)}, u32[]{:S(2)}, u32[]{:S(2)}) collective-permute-start(f32[26,1,128]{2,1,0:T(1,128)S(1)} %get-tuple-element.26), channel_id=1, source_target_pairs={{0,1},{1,2},{2,3},{3,4},{4,5},{5,6},{6,7},{7,8},{8,9},{9,10},{10,1... | collective-permute-start | bytes 39944 | tf_op jit(solution)/shard_map/ppermute | solution.py:21
  22.6 15.1 %collective-permute-start.3 = (f32[26,1,128]{2,1,0:T(1,128)S(1)}, f32[26,1,128]{2,1,0:T(1,128)S(1)}, u32[]{:S(2)}, u32[]{:S(2)}) collective-permute-start(f32[26,1,128]{2,1,0:T(1,128)S(1)} %get-tuple-element.27), channel_id=1, source_target_pairs={{1,0},{2,1},{3,2},{4,3},{5,4},{6,5},{7,6},{8,7},{9,8},{10,9},{11,1... | collective-permute-start | bytes 39944 | tf_op jit(solution)/shard_map/ppermute | solution.py:23
  38.2 20.4 %copy-start.11 = (f32[3,10]{1,0:T(4,128)S(1)}, f32[3,10]{1,0:T(4,128)}, u32[]{:S(2)}) copy-start(f32[3,10]{1,0:T(4,128)} %param.16) | copy-start | bytes 364
  38.2 20.4 %copy-start.21 = (f32[1,10]{1,0:T(1,128)S(1)}, f32[1,10]{1,0:T(1,128)}, u32[]{:S(2)}) copy-start(f32[1,10]{1,0:T(1,128)} %param.17) | copy-start | bytes 124
  38.3 5.0 %collective-permute-start.4 = (f32[2,8,128]{2,1,0:T(8,128)S(1)}, f32[2,8,128]{2,1,0:T(8,128)S(1)}, u32[]{:S(2)}, u32[]{:S(2)}) collective-permute-start(f32[2,8,128]{2,1,0:T(8,128)S(1)} %get-tuple-element.14), channel_id=1, source_target_pairs={{0,128},{128,256},{256,384},{384,512},{512,640},{640,768},{768,896... | collective-permute-start | bytes 24584 | tf_op jit(solution)/shard_map/ppermute | solution.py:21
  41.1 18.7 %copy-start.10 = (f32[16,10]{1,0:T(8,128)S(1)}, f32[16,10]{1,0:T(8,128)}, u32[]{:S(2)}) copy-start(f32[16,10]{1,0:T(8,128)} %param.18) | copy-start | bytes 1924
  41.2 7.1 %collective-permute-start.5 = (f32[2,8,128]{2,1,0:T(8,128)S(1)}, f32[2,8,128]{2,1,0:T(8,128)S(1)}, u32[]{:S(2)}, u32[]{:S(2)}) collective-permute-start(f32[2,8,128]{2,1,0:T(8,128)S(1)} %get-tuple-element.15), channel_id=1, source_target_pairs={{128,0},{256,128},{384,256},{512,384},{640,512},{768,640},{896,768... | collective-permute-start | bytes 24584 | tf_op jit(solution)/shard_map/ppermute | solution.py:23
  43.3 17.6 %copy-start.1 = (f32[24,8,128]{2,1,0:T(8,128)}, f32[24,8,128]{2,1,0:T(8,128)S(1)}, u32[]{:S(2)}) copy-start(f32[24,8,128]{2,1,0:T(8,128)S(1)} %slice.201) | copy-start | bytes 294916
  48.3 12.3 %collective-permute-start.6 = (f32[28,2,128]{2,1,0:T(2,128)S(1)}, f32[28,2,128]{2,1,0:T(2,128)S(1)}, u32[]{:S(2)}, u32[]{:S(2)}) collective-permute-start(f32[28,2,128]{2,1,0:T(2,128)S(1)} %get-tuple-element.22), channel_id=1, source_target_pairs={{0,1},{1,2},{2,3},{3,4},{4,5},{5,6},{6,7},{7,8},{8,9},{9,10},{10,1... | collective-permute-start | bytes 86024 | tf_op jit(solution)/shard_map/ppermute | solution.py:21
  50.2 10.4 %collective-permute-start.7 = (f32[28,2,128]{2,1,0:T(2,128)S(1)}, f32[28,2,128]{2,1,0:T(2,128)S(1)}, u32[]{:S(2)}, u32[]{:S(2)}) collective-permute-start(f32[28,2,128]{2,1,0:T(2,128)S(1)} %get-tuple-element.23), channel_id=1, source_target_pairs={{1,0},{2,1},{3,2},{4,3},{5,4},{6,5},{7,6},{8,7},{9,8},{10,9},{11,1... | collective-permute-start | bytes 86024 | tf_op jit(solution)/shard_map/ppermute | solution.py:23
  78.1 4.8 %collective-permute-start.8 = (f32[1,8,128]{2,1,0:T(8,128)S(1)}, f32[1,8,128]{2,1,0:T(8,128)S(1)}, u32[]{:S(2)}, u32[]{:S(2)}) collective-permute-start(f32[1,8,128]{2,1,0:T(8,128)S(1)} %copy.112), channel_id=1, source_target_pairs={{0,128},{128,256},{256,384},{384,512},{512,640},{640,768},{768,896... | collective-permute-start | bytes 12296 | tf_op jit(solution)/shard_map/ppermute | solution.py:21
  80.4 17.6 %copy-start.17 = (pred[26]{0:T(512)(128)(4,1)S(1)}, pred[26]{0:T(512)(128)(4,1)}, u32[]{:S(2)}) copy-start(pred[26]{0:T(512)(128)(4,1)} %copy-done.16) | copy-start | bytes 82
  80.4 17.7 %copy-start.19 = (pred[26]{0:T(512)(128)(4,1)S(1)}, pred[26]{0:T(512)(128)(4,1)}, u32[]{:S(2)}) copy-start(pred[26]{0:T(512)(128)(4,1)} %copy-done.18) | copy-start | bytes 82
  80.4 7.2 %collective-permute-start.9 = (f32[1,8,128]{2,1,0:T(8,128)S(1)}, f32[1,8,128]{2,1,0:T(8,128)S(1)}, u32[]{:S(2)}, u32[]{:S(2)}) collective-permute-start(f32[1,8,128]{2,1,0:T(8,128)S(1)} %copy.115), channel_id=1, source_target_pairs={{128,0},{256,128},{384,256},{512,384},{640,512},{768,640},{896,768... | collective-permute-start | bytes 12296 | tf_op jit(solution)/shard_map/ppermute | solution.py:23
  87.6 9.5 %collective-permute-start.10 = (f32[26,1,128]{2,1,0:T(1,128)S(1)}, f32[26,1,128]{2,1,0:T(1,128)S(1)}, u32[]{:S(2)}, u32[]{:S(2)}) collective-permute-start(f32[26,1,128]{2,1,0:T(1,128)S(1)} %get-tuple-element.24), channel_id=1, source_target_pairs={{0,1},{1,2},{2,3},{3,4},{4,5},{5,6},{6,7},{7,8},{8,9},{9,10},{10,1... | collective-permute-start | bytes 39944 | tf_op jit(solution)/shard_map/ppermute | solution.py:21
  89.5 8.7 %copy-start.13 = (pred[10]{0:T(512)(128)(4,1)S(1)}, pred[10]{0:T(512)(128)(4,1)}, u32[]{:S(2)}) copy-start(pred[10]{0:T(512)(128)(4,1)} %copy-done.12) | copy-start | bytes 34
  89.6 8.4 %collective-permute-start.11 = (f32[26,1,128]{2,1,0:T(1,128)S(1)}, f32[26,1,128]{2,1,0:T(1,128)S(1)}, u32[]{:S(2)}, u32[]{:S(2)}) collective-permute-start(f32[26,1,128]{2,1,0:T(1,128)S(1)} %get-tuple-element.25), channel_id=1, source_target_pairs={{1,0},{2,1},{3,2},{4,3},{5,4},{6,5},{7,6},{8,7},{9,8},{10,9},{11,1... | collective-permute-start | bytes 39944 | tf_op jit(solution)/shard_map/ppermute | solution.py:23
  (10 other events, 24.2 us)
where the time goes:
time: 99.8 us; the launch traced here: 99.2 us
  starting transfers between devices  56.2 us (56%)
  waiting for transfers between devices  16.2 us (16%)
  local copies, waits for them, and re-layouts  11 us (11%)
  matrix products  9.13 us (9%)
  other arithmetic  5.19 us (5%)
  between operations  1.51 us (2%)
    ppermute x6, starting transfers between devices, padded_2(): lax.ppermute(head, axis, [((i + 1) % count, i) for i in range(ends)])  36.2 us
    ppermute x6, starting transfers between devices, padded_2(): lax.ppermute(tail, axis, [(i, (i + 1) % count) for i in range(ends)])  20 us
    ppermute x6, waiting for transfers between devices, padded_2(): lax.ppermute(head, axis, [((i + 1) % count, i) for i in range(ends)])  16.1 us
    dot_general x1, matrix products, modal_first(): result = jnp.einsum('amp,amyz->apyz', modes, shaped, precision=HIGHEST)  4.66 us
    another operation x1, local copies, waits for them, and re-layouts, modal_first(): shaped = source.reshape(blocks, extent, source.shape[1], source.shape[2])  3.02 us
  transfers between devices with their start and end apart: 12, of which 5 were waited for; matrix products, arithmetic and copies ran while one was open for 3% of the time, Pallas kernels for 0%

commit v1 on v0

v1 whole, which is shorter than its diff:
```python
import jax
import jax.numpy as jnp
import numpy as np
from jax import lax
from jax.experimental import pallas as pl
from jax.experimental.pallas import tpu as pltpu
from jax.sharding import PartitionSpec as P

N1 = 8
M = 10
AB = 3
CB = 16
NF = AB * N1
OWN = NF * N1
HALO = 192
COLS = OWN + HALO
STEP = 104
ROWS = 320
DEEP = 384
WIDE = 256
F32 = jnp.float32
BF16 = jnp.bfloat16
HIGHEST = lax.Precision.HIGHEST
MESH = pl.DeviceIdType.MESH

SLOTS = ((0, -1), (0, 1), (-1, 0), (1, 0), (-1, -1), (-1, 1), (1, -1), (1, 1))
FIRST_AT = (0, 48, 96, 112, 128, 144, 160, 176)
FIRST_LEN = (48, 48, 16, 16, 16, 16, 16, 16)
LAST_AT = (0, 24, 48, 56, 64, 72, 80, 88)
LAST_LEN = (24, 24, 8, 8, 8, 8, 8, 8)
LAST_FROM = (0, 24, 48, 56, 48, 48, 56, 56)


def legendre_values(nodes, degree):
    table = np.zeros((nodes.shape[0], degree + 1))
    table[:, 0] = 1.0
    table[:, 1] = nodes
    for order in range(2, degree + 1):
        table[:, order] = (
            (2 * order - 1) * nodes * table[:, order - 1] - (order - 1) * table[:, order - 2]
        ) / order
    return table


def derivative_table(points):
    degree = points - 1
    nodes = np.cos(np.pi * np.arange(points) / degree)
    for sweep in range(100):
        table = legendre_values(nodes, degree)
        nodes = nodes - (nodes * table[:, degree] - table[:, degree - 1]) / (
            points * table[:, degree]
        )
    gll_nodes = nodes[::-1]
    legendre_at = legendre_values(gll_nodes, degree)[:, degree]
    diff_table = np.zeros((points, points))
    for first_index in range(points):
        for second_index in range(points):
            if first_index != second_index:
                diff_table[first_index, second_index] = legendre_at[first_index] / (
                    legendre_at[second_index] * (gll_nodes[first_index] - gll_nodes[second_index])
                )
    diff_table[0, 0] = -degree * (degree + 1) / 4.0
    diff_table[degree, degree] = degree * (degree + 1) / 4.0
    return diff_table


LAYER_NODE = [0, 1, 1, 2, 3, 4, 5, 6, 7, 8, 8, 9]


def tables():
    diff = derivative_table(N1).astype(np.float32)
    eye8 = np.eye(N1, dtype=np.float32)
    left = np.concatenate([np.kron(diff, eye8), np.kron(eye8, diff)], axis=0)
    third = np.kron(np.eye(CB, dtype=np.float32), diff.T)
    gather = np.zeros((CB * N1, WIDE), np.float32)
    scatter = np.zeros((WIDE, CB * N1), np.float32)
    for c in range(CB):
        for layer in range(12):
            at = c * N1 + layer - 2
            if 0 <= at < CB * N1:
                gather[at, LAYER_NODE[layer] * 16 + c] = 1.0
                if 0 < layer < 11:
                    scatter[LAYER_NODE[layer] * 16 + c, at] = 1.0
    pick_p = np.zeros((ROWS, 128), np.float32)
    pick_q = np.zeros((ROWS, 128), np.float32)
    for a in range(AB):
        for p in range(M):
            for q in range(M):
                pick_p[a * STEP + p * M + q, p] = 1.0
                pick_q[a * STEP + p * M + q, q] = 1.0
    first_layer = np.zeros(COLS, np.int32)
    second_layer = np.full(COLS, -1, np.int32)
    for f in range(NF):
        for j in range(N1):
            first_layer[f * N1 + j] = f + 2
            second_layer[f * N1 + j] = j + 2
    for slot, (side_s, side_c) in enumerate(SLOTS):
        for row in range(FIRST_LEN[slot]):
            col = OWN + FIRST_AT[slot] + row
            if side_s == 0:
                jj, f = divmod(row, NF)
                first_layer[col] = f + 2
                second_layer[col] = jj if side_c < 0 else 10 + jj
            else:
                l, j = divmod(row, N1)
                first_layer[col] = l if side_s < 0 else 26 + l
                if side_c == 0:
                    second_layer[col] = j + 2
                elif side_c < 0:
                    second_layer[col] = j - 6 if j >= 6 else -1
                else:
                    second_layer[col] = 10 + j if j < 2 else -1
    cols_first = np.zeros((128, COLS), np.float32)
    cols_second = np.zeros((128, COLS), np.float32)
    for col in range(COLS):
        for a in range(AB):
            layer = first_layer[col] - N1 * a
            if 0 <= layer < 12:
                cols_first[LAYER_NODE[layer] * 8 + a, col] = 1.0
        if second_layer[col] >= 0:
            cols_second[LAYER_NODE[second_layer[col]] * 8 + 3, col] = 1.0
    exact = [gather, scatter, pick_p, pick_q, cols_first, cols_second]
    return [left, left.T.copy(), third, third.T.copy()] + [t.astype(BF16) for t in exact]


def dot(a, b):
    return lax.dot_general(a, b, (((1,), (0,)), ((), ())), preferred_element_type=F32)


def split(value):
    high = value.astype(BF16)
    return high, (value - high.astype(F32)).astype(BF16)


def product(a, b):
    return dot(a[0], b[0]) + (dot(a[1], b[0]) + dot(a[0], b[1]))


def select(table, value):
    high, low = split(value)
    return dot(table, high), dot(table, low)


def iota(shape, dimension):
    return lax.broadcasted_iota(jnp.int32, shape, dimension)


def block_of(rows):
    return (rows >= STEP).astype(jnp.int32) + (rows >= 2 * STEP).astype(jnp.int32)


def kernel(*refs):
    hbm = refs[:19]
    op_ref, pre_ref = refs[19:21]
    vmem = refs[21:40]
    (
        own,
        stage,
        halo,
        stage_last,
        halo_last,
        assembled,
        solved,
        kept,
        modes3,
        modes12,
        eigen,
        load_sem,
        send_sem,
        recv_sem,
        send_last,
        recv_last,
    ) = refs[40:]
    (
        pressure,
        geo_diag,
        geo_off,
        modes_first,
        modes_second,
        modes_third,
        eigen_first,
        eigen_second,
        eigen_third,
        left,
        left_t,
        third,
        third_t,
        gather,
        scatter,
        pick_p,
        pick_q,
        cols_first,
        cols_second,
    ) = vmem
    n_s, n_c = lax.axis_size("stream"), lax.axis_size("cross")
    me_s, me_c = lax.axis_index("stream"), lax.axis_index("cross")

    def peer(side_s, side_c):
        return {
            "stream": lax.rem(me_s + side_s + n_s, n_s),
            "cross": lax.rem(me_c + side_c + n_c, n_c),
        }

    barrier = pltpu.get_barrier_semaphore()
    for side_s, side_c in SLOTS:
        pl.semaphore_signal(barrier, inc=1, device_id=peer(side_s, side_c), device_id_type=MESH)
    loads = [
        pltpu.make_async_copy(hbm[i], vmem[i], load_sem.at[i]) for i in range(19)
    ]
    order = [0, 9, 11, 1, 2, 10, 12, 3, 4, 5, 6, 7, 8, 13, 14, 15, 16, 17, 18]
    for i in order:
        loads[i].start()

    modes3[...] = jnp.zeros_like(modes3)
    modes12[...] = jnp.zeros_like(modes12)
    eigen[...] = jnp.zeros_like(eigen)

    for i in (0, 9, 11):
        loads[i].wait()
    pres = pressure[...].reshape(OWN, 128)
    pres_split = split(pres)
    left_split = split(left[...])
    third_split = split(third[...])
    per = N1 * N1
    along = [
        product(left_split, tuple(part[a * per : (a + 1) * per] for part in pres_split))
        for a in range(AB)
    ]
    grad_third = product(pres_split, third_split)
    for i in (1, 2, 10, 12):
        loads[i].wait()
    left_t_split = split(left_t[...])
    third_t_split = split(third_t[...])
    for a in range(AB):
        rows = pl.ds(a * N1, N1)
        d0, d1, d2 = (geo_diag[k, rows].reshape(per, 128) for k in range(3))
        o0, o1, o2 = (geo_off[k, rows].reshape(per, 128) for k in range(3))
        g1, g2 = along[a][:per], along[a][per:]
        g3 = grad_third[a * per : (a + 1) * per]
        flux_first = d0 * g1 + o0 * g2 + o1 * g3
        flux_second = o0 * g1 + d1 * g2 + o2 * g3
        flux_third = o1 * g1 + o2 * g2 + d2 * g3
        both = split(jnp.concatenate([flux_first, flux_second], axis=0))
        own[pl.ds(a * per, per), :] = product(left_t_split, both) + product(
            split(flux_third), third_t_split
        )
    for k, node in enumerate((6, 7, 0, 1)):
        stage[pl.ds(k * NF, NF), :] = own[pl.ds(node, NF, stride=N1), :]

    pl.semaphore_wait(barrier, len(SLOTS))
    first_from = (
        stage.at[pl.ds(0, 48), :],
        stage.at[pl.ds(48, 48), :],
        own.at[pl.ds(OWN - 16, 16), :],
        own.at[pl.ds(0, 16), :],
        own.at[pl.ds(OWN - 16, 16), :],
        own.at[pl.ds(OWN - 16, 16), :],
        own.at[pl.ds(0, 16), :],
        own.at[pl.ds(0, 16), :],
    )
    sends = {}
    for slot in (4, 5, 6, 7, 0, 1, 2, 3):
        side_s, side_c = SLOTS[slot]
        sends[slot] = pltpu.make_async_remote_copy(
            src_ref=first_from[slot],
            dst_ref=halo.at[pl.ds(FIRST_AT[slot], FIRST_LEN[slot]), :],
            send_sem=send_sem.at[slot],
            recv_sem=recv_sem.at[slot],
            device_id=peer(-side_s, -side_c),
            device_id_type=MESH,
        )
        sends[slot].start()

    at_s = {-1: me_s > 0, 1: me_s < n_s - 1}
    at_c = {-1: me_c > 0, 1: me_c < n_c - 1}

    def there(slot):
        side_s, side_c = SLOTS[slot]
        if side_s == 0:
            return at_c[side_c]
        if side_c == 0:
            return at_s[side_s]
        return jnp.logical_and(at_s[side_s], at_c[side_c])

    for i in (3, 4, 5, 6, 7, 8, 13, 14, 15, 16, 17, 18):
        loads[i].wait()
    for m in range(M):
        modes3[m * 16 : m * 16 + CB, 0:M] = modes_third[m]
        modes12[m * 8 : m * 8 + AB, 0:M] = modes_first[m]
        modes12[m * 8 + 3 : m * 8 + 4, 0:M] = modes_second[m]
    eigen[0:AB, 0:M] = eigen_first[...]
    eigen[8:9, 0:M] = eigen_second[...]
    eigen[16 : 16 + CB, 0:M] = eigen_third[...]

    spread = jnp.where(iota((128, WIDE), 0) == (iota((128, WIDE), 1) & 15), 1.0, 0.0).astype(F32)
    diagonal = jnp.dot(modes3[...], spread, precision=HIGHEST, preferred_element_type=F32)
    same = (iota((WIDE, WIDE), 0) & 15) == (iota((WIDE, WIDE), 1) >> 4)
    diagonal = jnp.where(same, diagonal, 0.0)
    fore = tuple(part.astype(BF16) for part in select(gather[...], diagonal))
    back = []
    for part in split(jnp.transpose(diagonal)):
        back.append(dot(part, scatter[...]).astype(BF16))

    take_p = pick_p[...].astype(F32)
    take_q = pick_q[...].astype(F32)
    nt = (((1,), (1,)), ((), ()))
    by_p = lax.dot_general(take_p, modes12[...], nt, precision=HIGHEST, preferred_element_type=F32)
    by_q = lax.dot_general(take_q, modes12[...], nt, precision=HIGHEST, preferred_element_type=F32)
    by_p = jnp.where(block_of(iota((ROWS, 128), 0)) == (iota((ROWS, 128), 1) & 7), by_p, 0.0)
    by_p_split, by_q_split = split(by_p), split(by_q)
    forward = (dot(by_p_split[0], cols_first[...]) + dot(by_p_split[1], cols_first[...])) * (
        dot(by_q_split[0], cols_second[...]) + dot(by_q_split[1], cols_second[...])
    )
    forward_own = forward[:, :OWN]
    cols = iota((1, COLS), 1)
    absent = jnp.zeros((1, COLS), jnp.int32)
    for slot in range(len(SLOTS)):
        begin = OWN + FIRST_AT[slot]
        inside = jnp.logical_and(cols >= begin, cols < begin + FIRST_LEN[slot])
        missing = 1 - there(slot).astype(jnp.int32)
        absent = absent + jnp.where(inside, missing, 0)
    forward_halo = jnp.where(absent > 0, 0.0, forward)[:, OWN:]
    own_split = split(forward_own)
    halo_split = split(forward_halo)

    relative = (iota((ROWS, WIDE), 1) >> 3) + 2 - N1 * block_of(iota((ROWS, WIDE), 0))
    keep = jnp.logical_and(relative != 0, relative != 11)
    square = jnp.where(keep, forward[:, :WIDE], 0.0)
    square = jnp.concatenate([square, jnp.zeros((DEEP - ROWS, WIDE), F32)], axis=0)
    kept[...] = jnp.transpose(square)
    back_own = split(kept[pl.ds(0, OWN), :])
    back_edge = split(
        jnp.concatenate(
            [
                kept[pl.ds(0, 8), :],
                kept[pl.ds(OWN - 8, 8), :],
            ],
            axis=0,
        )
    )
    back_far = split(
        jnp.concatenate(
            [kept[pl.ds(7 + 8 * f, 1), :] for f in range(NF)]
            + [kept[pl.ds(8 * f, 1), :] for f in range(NF)],
            axis=0,
        )
    )

    third_eigen = jnp.dot(
        eigen[16 : 16 + CB, :], spread, precision=HIGHEST, preferred_element_type=F32
    )
    third_eigen = jnp.where(
        iota((CB, WIDE), 0) == (iota((CB, WIDE), 1) >> 4), third_eigen, 0.0
    )
    lane_part = jnp.sum(third_eigen, axis=0, keepdims=True)
    inverse = []
    edges = [0, STEP, 2 * STEP, ROWS]
    for a in range(AB):
        rows = slice(edges[a], edges[a + 1])
        row_part = jnp.sum(
            take_p[rows] * eigen[a : a + 1, :] + take_q[rows] * eigen[8:9, :],
            axis=1,
            keepdims=True,
        )
        total = row_part + lane_part
        inverse.append(1.0 / jnp.where(total > 0.0, total, 1.0))
    inverse = jnp.concatenate(inverse, axis=0)

    own_third = product(split(own[...]), fore)
    spectral_own = product(own_split, split(own_third))

    for slot in range(len(SLOTS)):
        sends[slot].wait_recv()
    halo_third = product(split(halo[...]), fore)
    spectral = (spectral_own + product(halo_split, split(halo_third))) * inverse
    spectral = split(
        jnp.concatenate([spectral, jnp.zeros((DEEP - ROWS, WIDE), F32)], axis=0)
    )
    stage_last[pl.ds(0, 48), :] = product(split(product(back_far, spectral)), back)
    edge = product(split(product(back_edge, spectral)), back)
    stage_last[pl.ds(48, 8), :] = edge[8:16]
    stage_last[pl.ds(56, 8), :] = edge[0:8]
    last = {}
    for slot in (4, 5, 6, 7, 0, 1, 2, 3):
        side_s, side_c = SLOTS[slot]
        last[slot] = pltpu.make_async_remote_copy(
            src_ref=stage_last.at[pl.ds(LAST_FROM[slot], LAST_LEN[slot]), :],
            dst_ref=halo_last.at[pl.ds(LAST_AT[slot], LAST_LEN[slot]), :],
            send_sem=send_last.at[slot],
            recv_sem=recv_last.at[slot],
            device_id=peer(-side_s, -side_c),
            device_id_type=MESH,
        )
        last[slot].start()

    sub = iota((8, 128), 0)

    def shifted(tile, to_top):
        moved = pltpu.roll(tile, 1 if to_top else 7, 0)
        return jnp.where(sub == (0 if to_top else 7), moved, 0.0)

    assembled[...] = own[...]
    for slot, node, row in ((0, 0, 24), (1, 7, 48)):
        place = pl.ds(node, NF, stride=N1)
        got = jnp.where(there(slot), halo[pl.ds(row, NF), :], 0.0)
        assembled[place, :] = assembled[place, :] + got

    def layer_beside(slot, at_prev, at_next, side):
        rows = 8 if side < 0 else 0
        base = jnp.where(there(slot), halo[pl.ds(FIRST_AT[slot] + rows, 8), :], 0.0)
        corner = halo[pl.ds(FIRST_AT[at_prev] + rows, 8), :]
        base = base + jnp.where(there(at_prev), shifted(corner, True), 0.0)
        corner = halo[pl.ds(FIRST_AT[at_next] + rows, 8), :]
        return base + jnp.where(there(at_next), shifted(corner, False), 0.0)

    assembled[pl.ds(0, 8), :] = assembled[pl.ds(0, 8), :] + layer_beside(2, 4, 5, -1)
    assembled[pl.ds(OWN - 8, 8), :] = assembled[pl.ds(OWN - 8, 8), :] + layer_beside(3, 6, 7, 1)
    for a in range(AB - 1):
        at = (a * N1 + 7) * N1
        total = assembled[pl.ds(at, 8), :] + assembled[pl.ds(at + 8, 8), :]
        assembled[pl.ds(at, 8), :] = total
        assembled[pl.ds(at + 8, 8), :] = total
    value = assembled[...]
    lane = iota((OWN, 128), 1)
    from_left = jnp.where(jnp.logical_and((lane & 7) == 0, lane > 0), pltpu.roll(value, 1, 1), 0.0)
    from_right = jnp.where(
        jnp.logical_and((lane & 7) == 7, lane < 127), pltpu.roll(value, 127, 1), 0.0
    )
    op_ref[...] = (value + from_left + from_right).reshape(NF, N1, 128)

    solved[...] = product(split(product(back_own, spectral)), back)

    for slot in range(len(SLOTS)):
        last[slot].wait_recv()
    for slot, node, row in ((0, 0, 0), (1, 7, 24)):
        place = pl.ds(node, NF, stride=N1)
        got = jnp.where(there(slot), halo_last[pl.ds(row, NF), :], 0.0)
        solved[place, :] = solved[place, :] + got

    def layer_last(slot, at_prev, at_next):
        base = jnp.where(there(slot), halo_last[pl.ds(LAST_AT[slot], 8), :], 0.0)
        corner = halo_last[pl.ds(LAST_AT[at_prev], 8), :]
        base = base + jnp.where(there(at_prev), shifted(corner, True), 0.0)
        corner = halo_last[pl.ds(LAST_AT[at_next], 8), :]
        return base + jnp.where(there(at_next), shifted(corner, False), 0.0)

    solved[pl.ds(0, 8), :] = solved[pl.ds(0, 8), :] + layer_last(2, 4, 5)
    solved[pl.ds(OWN - 8, 8), :] = solved[pl.ds(OWN - 8, 8), :] + layer_last(3, 6, 7)
    pre_ref[...] = solved[...].reshape(NF, N1, 128)

    for slot in range(len(SLOTS)):
        sends[slot].wait_send()
        last[slot].wait_send()


def shards(*args):
    operands = list(args) + [jnp.asarray(t) for t in tables()]
    for i in (3, 4, 5):
        operands[i] = jnp.transpose(operands[i], (1, 0, 2))
    out = jax.ShapeDtypeStruct((NF, N1, CB * N1), F32)
    return pl.pallas_call(
        kernel,
        out_shape=(out, out),
        in_specs=[pl.BlockSpec(memory_space=pl.ANY)] * len(operands),
        out_specs=(pl.BlockSpec(memory_space=pltpu.VMEM),) * 2,
        scratch_shapes=[pltpu.VMEM(t.shape, t.dtype) for t in operands]
        + [
            pltpu.VMEM((OWN, 128), F32),
            pltpu.VMEM((96, 128), F32),
            pltpu.VMEM((HALO, 128), F32),
            pltpu.VMEM((64, 128), F32),
            pltpu.VMEM((96, 128), F32),
            pltpu.VMEM((OWN, 128), F32),
            pltpu.VMEM((OWN, 128), F32),
            pltpu.VMEM((WIDE, DEEP), F32),
            pltpu.VMEM((WIDE, 128), F32),
            pltpu.VMEM((128, 128), F32),
            pltpu.VMEM((32, 128), F32),
            pltpu.SemaphoreType.DMA((19,)),
            pltpu.SemaphoreType.DMA((8,)),
            pltpu.SemaphoreType.DMA((8,)),
            pltpu.SemaphoreType.DMA((8,)),
            pltpu.SemaphoreType.DMA((8,)),
        ],
        compiler_params=pltpu.CompilerParams(collective_id=0, has_side_effects=True),
        name="pressure_step",
    )(*operands)


def solution(mesh):
    in_specs = (
        P("stream", "cross", None),
        P(None, "stream", "cross", None),
        P(None, "stream", "cross", None),
        P("stream", None, None),
        P("cross", None, None),
        P(),
        P("stream", None),
        P("cross", None),
        P(),
    )
    out_specs = (P("stream", "cross", None), P("stream", "cross", None))
    return jax.shard_map(shards, mesh=mesh, in_specs=in_specs, out_specs=out_specs, check_vma=False)
```

time: 99.8 us -> 39.9 us (0.40)
  the two profiles are of different devices: /device:TPU:41 before, /device:TPU:1 now
where the time goes in v1:
time: 39.9 us; the launch traced here: 39.7 us
  Pallas kernels  36.8 us (92%)
  local copies, waits for them, and re-layouts  2.22 us (6%)
  between operations  0.65 us (2%)
    pallas_call x1, Pallas kernels, shards(): pl.pallas_call(kernel, out_shape=(out, out), in_specs=[pl.BlockSpec(memor...  36.8 us
    unnamed x4, local copies, waits for them, and re-layouts  2.22 us

profile of v1, /device:TPU:1, one launch (start us, length us, event | category | flops | bytes accessed | tf_op | source)
XLA Modules:
  0.0 39.7 jit_solution(5844101953313832106)
XLA Ops:
  0.6 36.8 %pressure_step.1 = (f32[24,8,128]{2,1,0:T(8,128)}, f32[24,8,128]{2,1,0:T(8,128)}) custom-call(f32[24,8,128]{2,1,0:T(8,128)} %refs_0_.1, f32[3,24,8,128]{3,2,1,0:T(8,128)} %refs_1_.1, f32[3,24,8,128]{3,2,1,0:T(8,128)} %refs_2_.1, f32[10,3,10]{2,1,0:T(4,128)} %bitcast.4, f32[10,1,10]{2,1,0:T(1,128)} %bitcast.5, f32[10,16,10]{2,1,0:T(8,128)} %bitcast.3, ...), custom_call_target="tpu_custom_call" | custom-call | tf_op jit(solution)/shard_map/pressure_step/pallas_call | solution.py:461
  37.5 0.0 copy-start
  37.5 1.6 %copy.23 = f32[24,8,128]{2,1,0:T(8,128)} copy(f32[24,8,128]{2,1,0:T(8,128)} %get-tuple-element.4) | data formatting | bytes 196608
  39.1 0.0 copy-done
  39.1 0.6 %copy.24 = f32[24,8,128]{2,1,0:T(8,128)} copy(f32[24,8,128]{2,1,0:T(8,128)S(1)} %copy-done) | data formatting | bytes 196608
Async XLA Ops:
  37.5 1.6 %copy-start = (f32[24,8,128]{2,1,0:T(8,128)S(1)}, f32[24,8,128]{2,1,0:T(8,128)}, u32[]{:S(2)}) copy-start(f32[24,8,128]{2,1,0:T(8,128)} %get-tuple-element.5) | copy-start | bytes 294916

commit v2 on v1

--- a/solution.py
+++ b/solution.py
@@ -1,3 +1,5 @@
+import functools
+
 import jax
 import jax.numpy as jnp
 import numpy as np
@@ -29,6 +31,7 @@
 LAST_AT = (0, 24, 48, 56, 64, 72, 80, 88)
 LAST_LEN = (24, 24, 8, 8, 8, 8, 8, 8)
 LAST_FROM = (0, 24, 48, 56, 48, 48, 56, 56)
+FAR_FIRST = (4, 5, 6, 7, 0, 1, 2, 3)
 
 
 def legendre_values(nodes, degree):
@@ -201,9 +204,32 @@
             "cross": lax.rem(me_c + side_c + n_c, n_c),
         }
 
+    at_s = {-1: me_s > 0, 0: True, 1: me_s < n_s - 1}
+    at_c = {-1: me_c > 0, 0: True, 1: me_c < n_c - 1}
+
+    def there(side_s, side_c):
+        if side_s == 0:
+            return at_c[side_c]
+        if side_c == 0:
+            return at_s[side_s]
+        return jnp.logical_and(at_s[side_s], at_c[side_c])
+
+    def for_each(order, sign, act):
+        for slot in order:
+            side_s, side_c = SLOTS[slot]
+            pl.when(there(sign * side_s, sign * side_c))(functools.partial(act, slot))
+
+    halo[...] = jnp.zeros_like(halo)
+    halo_last[...] = jnp.zeros_like(halo_last)
     barrier = pltpu.get_barrier_semaphore()
-    for side_s, side_c in SLOTS:
-        pl.semaphore_signal(barrier, inc=1, device_id=peer(side_s, side_c), device_id_type=MESH)
+
+    def greet(slot):
+        pl.semaphore_signal(barrier, inc=1, device_id=peer(*SLOTS[slot]), device_id_type=MESH)
+
+    for_each(range(8), 1, greet)
+    count_s = at_s[-1].astype(jnp.int32) + at_s[1].astype(jnp.int32)
+    count_c = at_c[-1].astype(jnp.int32) + at_c[1].astype(jnp.int32)
+    neighbours = count_s + count_c + count_s * count_c
     loads = [
         pltpu.make_async_copy(hbm[i], vmem[i], load_sem.at[i]) for i in range(19)
     ]
@@ -247,7 +273,7 @@
     for k, node in enumerate((6, 7, 0, 1)):
         stage[pl.ds(k * NF, NF), :] = own[pl.ds(node, NF, stride=N1), :]
 
-    pl.semaphore_wait(barrier, len(SLOTS))
+    pl.semaphore_wait(barrier, neighbours)
     first_from = (
         stage.at[pl.ds(0, 48), :],
         stage.at[pl.ds(48, 48), :],
@@ -259,8 +285,7 @@
         own.at[pl.ds(0, 16), :],
     )
     sends = {}
-    for slot in (4, 5, 6, 7, 0, 1, 2, 3):
-        side_s, side_c = SLOTS[slot]
+    for slot, (side_s, side_c) in enumerate(SLOTS):
         sends[slot] = pltpu.make_async_remote_copy(
             src_ref=first_from[slot],
             dst_ref=halo.at[pl.ds(FIRST_AT[slot], FIRST_LEN[slot]), :],
@@ -269,18 +294,7 @@
             device_id=peer(-side_s, -side_c),
             device_id_type=MESH,
         )
-        sends[slot].start()
-
-    at_s = {-1: me_s > 0, 1: me_s < n_s - 1}
-    at_c = {-1: me_c > 0, 1: me_c < n_c - 1}
-
-    def there(slot):
-        side_s, side_c = SLOTS[slot]
-        if side_s == 0:
-            return at_c[side_c]
-        if side_c == 0:
-            return at_s[side_s]
-        return jnp.logical_and(at_s[side_s], at_c[side_c])
+    for_each(FAR_FIRST, -1, lambda slot: sends[slot].start())
 
     for i in (3, 4, 5, 6, 7, 8, 13, 14, 15, 16, 17, 18):
         loads[i].wait()
@@ -312,14 +326,7 @@
         dot(by_q_split[0], cols_second[...]) + dot(by_q_split[1], cols_second[...])
     )
     forward_own = forward[:, :OWN]
-    cols = iota((1, COLS), 1)
-    absent = jnp.zeros((1, COLS), jnp.int32)
-    for slot in range(len(SLOTS)):
-        begin = OWN + FIRST_AT[slot]
-        inside = jnp.logical_and(cols >= begin, cols < begin + FIRST_LEN[slot])
-        missing = 1 - there(slot).astype(jnp.int32)
-        absent = absent + jnp.where(inside, missing, 0)
-    forward_halo = jnp.where(absent > 0, 0.0, forward)[:, OWN:]
+    forward_halo = forward[:, OWN:]
     own_split = split(forward_own)
     halo_split = split(forward_halo)
 
@@ -369,8 +376,7 @@
     own_third = product(split(own[...]), fore)
     spectral_own = product(own_split, split(own_third))
 
-    for slot in range(len(SLOTS)):
-        sends[slot].wait_recv()
+    for_each(range(8), 1, lambda slot: sends[slot].wait_recv())
     halo_third = product(split(halo[...]), fore)
     spectral = (spectral_own + product(halo_split, split(halo_third))) * inverse
     spectral = split(
@@ -381,8 +387,7 @@
     stage_last[pl.ds(48, 8), :] = edge[8:16]
     stage_last[pl.ds(56, 8), :] = edge[0:8]
     last = {}
-    for slot in (4, 5, 6, 7, 0, 1, 2, 3):
-        side_s, side_c = SLOTS[slot]
+    for slot, (side_s, side_c) in enumerate(SLOTS):
         last[slot] = pltpu.make_async_remote_copy(
             src_ref=stage_last.at[pl.ds(LAST_FROM[slot], LAST_LEN[slot]), :],
             dst_ref=halo_last.at[pl.ds(LAST_AT[slot], LAST_LEN[slot]), :],
@@ -391,7 +396,7 @@
             device_id=peer(-side_s, -side_c),
             device_id_type=MESH,
         )
-        last[slot].start()
+    for_each(FAR_FIRST, -1, lambda slot: last[slot].start())
 
     sub = iota((8, 128), 0)
 
@@ -400,18 +405,15 @@
         return jnp.where(sub == (0 if to_top else 7), moved, 0.0)
 
     assembled[...] = own[...]
-    for slot, node, row in ((0, 0, 24), (1, 7, 48)):
+    for node, row in ((0, 24), (7, 48)):
         place = pl.ds(node, NF, stride=N1)
-        got = jnp.where(there(slot), halo[pl.ds(row, NF), :], 0.0)
-        assembled[place, :] = assembled[place, :] + got
+        assembled[place, :] = assembled[place, :] + halo[pl.ds(row, NF), :]
 
     def layer_beside(slot, at_prev, at_next, side):
         rows = 8 if side < 0 else 0
-        base = jnp.where(there(slot), halo[pl.ds(FIRST_AT[slot] + rows, 8), :], 0.0)
-        corner = halo[pl.ds(FIRST_AT[at_prev] + rows, 8), :]
-        base = base + jnp.where(there(at_prev), shifted(corner, True), 0.0)
-        corner = halo[pl.ds(FIRST_AT[at_next] + rows, 8), :]
-        return base + jnp.where(there(at_next), shifted(corner, False), 0.0)
+        base = halo[pl.ds(FIRST_AT[slot] + rows, 8), :]
+        base = base + shifted(halo[pl.ds(FIRST_AT[at_prev] + rows, 8), :], True)
+        return base + shifted(halo[pl.ds(FIRST_AT[at_next] + rows, 8), :], False)
 
     assembled[pl.ds(0, 8), :] = assembled[pl.ds(0, 8), :] + layer_beside(2, 4, 5, -1)
     assembled[pl.ds(OWN - 8, 8), :] = assembled[pl.ds(OWN - 8, 8), :] + layer_beside(3, 6, 7, 1)
@@ -430,27 +432,22 @@
 
     solved[...] = product(split(product(back_own, spectral)), back)
 
-    for slot in range(len(SLOTS)):
-        last[slot].wait_recv()
-    for slot, node, row in ((0, 0, 0), (1, 7, 24)):
+    for_each(range(8), 1, lambda slot: last[slot].wait_recv())
+    for node, row in ((0, 0), (7, 24)):
         place = pl.ds(node, NF, stride=N1)
-        got = jnp.where(there(slot), halo_last[pl.ds(row, NF), :], 0.0)
-        solved[place, :] = solved[place, :] + got
+        solved[place, :] = solved[place, :] + halo_last[pl.ds(row, NF), :]
 
     def layer_last(slot, at_prev, at_next):
-        base = jnp.where(there(slot), halo_last[pl.ds(LAST_AT[slot], 8), :], 0.0)
-        corner = halo_last[pl.ds(LAST_AT[at_prev], 8), :]
-        base = base + jnp.where(there(at_prev), shifted(corner, True), 0.0)
-        corner = halo_last[pl.ds(LAST_AT[at_next], 8), :]
-        return base + jnp.where(there(at_next), shifted(corner, False), 0.0)
+        base = halo_last[pl.ds(LAST_AT[slot], 8), :]
+        base = base + shifted(halo_last[pl.ds(LAST_AT[at_prev], 8), :], True)
+        return base + shifted(halo_last[pl.ds(LAST_AT[at_next], 8), :], False)
 
     solved[pl.ds(0, 8), :] = solved[pl.ds(0, 8), :] + layer_last(2, 4, 5)
     solved[pl.ds(OWN - 8, 8), :] = solved[pl.ds(OWN - 8, 8), :] + layer_last(3, 6, 7)
     pre_ref[...] = solved[...].reshape(NF, N1, 128)
 
-    for slot in range(len(SLOTS)):
-        sends[slot].wait_send()
-        last[slot].wait_send()
+    for_each(range(8), -1, lambda slot: sends[slot].wait_send())
+    for_each(range(8), -1, lambda slot: last[slot].wait_send())
 
 
 def shards(*args):

time: 39.9 us -> 37.4 us (0.937)
  the two profiles are of different devices: /device:TPU:1 before, /device:TPU:41 now
where the time goes in v2:
time: 37.4 us; the launch traced here: 37.2 us
  Pallas kernels  34.4 us (92%)
  local copies, waits for them, and re-layouts  2.22 us (6%)
  between operations  0.65 us (2%)
    pallas_call x1, Pallas kernels, shards(): pl.pallas_call(kernel, out_shape=(out, out), in_specs=[pl.BlockSpec(memor...  34.4 us
    unnamed x4, local copies, waits for them, and re-layouts  2.22 us

profile of v2, /device:TPU:41, one launch (start us, length us, event | category | flops | bytes accessed | tf_op | source)
XLA Modules:
  0.0 37.2 jit_solution(10434005042003553622)
XLA Ops:
  0.6 34.4 %pressure_step.1 = (f32[24,8,128]{2,1,0:T(8,128)}, f32[24,8,128]{2,1,0:T(8,128)}) custom-call(f32[24,8,128]{2,1,0:T(8,128)} %refs_0_.1, f32[3,24,8,128]{3,2,1,0:T(8,128)} %refs_1_.1, f32[3,24,8,128]{3,2,1,0:T(8,128)} %refs_2_.1, f32[10,3,10]{2,1,0:T(4,128)} %bitcast.4, f32[10,1,10]{2,1,0:T(1,128)} %bitcast.5, f32[10,16,10]{2,1,0:T(8,128)} %bitcast.3, ...), custom_call_target="tpu_custom_call" | custom-call | tf_op jit(solution)/shard_map/pressure_step/pallas_call | solution.py:458
  35.0 0.0 copy-start
  35.0 1.6 %copy.23 = f32[24,8,128]{2,1,0:T(8,128)} copy(f32[24,8,128]{2,1,0:T(8,128)} %get-tuple-element.4) | data formatting | bytes 196608
  36.6 0.0 copy-done
  36.6 0.6 %copy.24 = f32[24,8,128]{2,1,0:T(8,128)} copy(f32[24,8,128]{2,1,0:T(8,128)S(1)} %copy-done) | data formatting | bytes 196608
Async XLA Ops:
  35.0 1.6 %copy-start = (f32[24,8,128]{2,1,0:T(8,128)S(1)}, f32[24,8,128]{2,1,0:T(8,128)}, u32[]{:S(2)}) copy-start(f32[24,8,128]{2,1,0:T(8,128)} %get-tuple-element.5) | copy-start | bytes 294916

commit v3 on v2

--- a/solution.py
+++ b/solution.py
@@ -22,8 +22,8 @@
 WIDE = 256
 F32 = jnp.float32
 BF16 = jnp.bfloat16
-HIGHEST = lax.Precision.HIGHEST
 MESH = pl.DeviceIdType.MESH
+N_IN = 17
 
 SLOTS = ((0, -1), (0, 1), (-1, 0), (1, 0), (-1, -1), (-1, 1), (1, -1), (1, 1))
 FIRST_AT = (0, 48, 96, 112, 128, 144, 160, 176)
@@ -70,27 +70,35 @@
 LAYER_NODE = [0, 1, 1, 2, 3, 4, 5, 6, 7, 8, 8, 9]
 
 
+def halves(table):
+    high = table.astype(BF16)
+    return high, (table - high.astype(np.float32)).astype(BF16)
+
+
 def tables():
     diff = derivative_table(N1).astype(np.float32)
     eye8 = np.eye(N1, dtype=np.float32)
     left = np.concatenate([np.kron(diff, eye8), np.kron(eye8, diff)], axis=0)
-    third = np.kron(np.eye(CB, dtype=np.float32), diff.T)
-    gather = np.zeros((CB * N1, WIDE), np.float32)
-    scatter = np.zeros((WIDE, CB * N1), np.float32)
+    high, low = halves(left)
+    left_all = np.concatenate([high, high, low], axis=1)
+    left_t = np.concatenate([high.T, low.T], axis=1)
+    zero = np.zeros((CB * N1, CB * N1), BF16)
+    thirds = []
+    for matrix in (diff.T, diff):
+        high, low = halves(np.kron(np.eye(CB, dtype=np.float32), matrix))
+        thirds.append(np.block([[high, low], [high, zero]]))
+    gather = np.zeros((CB * N1, CB * M), np.float32)
     for c in range(CB):
         for layer in range(12):
             at = c * N1 + layer - 2
             if 0 <= at < CB * N1:
-                gather[at, LAYER_NODE[layer] * 16 + c] = 1.0
-                if 0 < layer < 11:
-                    scatter[LAYER_NODE[layer] * 16 + c, at] = 1.0
-    pick_p = np.zeros((ROWS, 128), np.float32)
-    pick_q = np.zeros((ROWS, 128), np.float32)
+                gather[at, LAYER_NODE[layer] * CB + c] = 1.0
+    pick = np.zeros((ROWS, 128), np.float32)
     for a in range(AB):
         for p in range(M):
             for q in range(M):
-                pick_p[a * STEP + p * M + q, p] = 1.0
-                pick_q[a * STEP + p * M + q, q] = 1.0
+                pick[a * STEP + p * M + q, p] = 1.0
+                pick[a * STEP + p * M + q, 64 + q] = 1.0
     first_layer = np.zeros(COLS, np.int32)
     second_layer = np.full(COLS, -1, np.int32)
     for f in range(NF):
@@ -122,8 +130,8 @@
                 cols_first[LAYER_NODE[layer] * 8 + a, col] = 1.0
         if second_layer[col] >= 0:
             cols_second[LAYER_NODE[second_layer[col]] * 8 + 3, col] = 1.0
-    exact = [gather, scatter, pick_p, pick_q, cols_first, cols_second]
-    return [left, left.T.copy(), third, third.T.copy()] + [t.astype(BF16) for t in exact]
+    exact = [t.astype(BF16) for t in (gather, pick, cols_first, cols_second)]
+    return [left_all, left_t] + thirds + exact
 
 
 def dot(a, b):
@@ -139,9 +147,20 @@
     return dot(a[0], b[0]) + (dot(a[1], b[0]) + dot(a[0], b[1]))
 
 
-def select(table, value):
-    high, low = split(value)
-    return dot(table, high), dot(table, low)
+def lane_product(a, table):
+    both = dot(jnp.concatenate(a, axis=1), table)
+    return both[:, :128] + both[:, 128:]
+
+
+def wide_product(a, b):
+    return dot(jnp.concatenate(a, axis=1), jnp.concatenate([b[0], b[0]], axis=0)) + dot(a[0], b[1])
+
+
+def product_nt(a, b):
+    def one(x, y):
+        return lax.dot_general(x, y, (((1,), (1,)), ((), ())), preferred_element_type=F32)
+
+    return one(a[0], b[0]) + (one(a[1], b[0]) + one(a[0], b[1]))
 
 
 def iota(shape, dimension):
@@ -153,9 +172,9 @@
 
 
 def kernel(*refs):
-    hbm = refs[:19]
-    op_ref, pre_ref = refs[19:21]
-    vmem = refs[21:40]
+    hbm = refs[:N_IN]
+    op_ref, pre_ref = refs[N_IN : N_IN + 2]
+    vmem = refs[N_IN + 2 : 2 * N_IN + 2]
     (
         own,
         stage,
@@ -173,7 +192,7 @@
         recv_sem,
         send_last,
         recv_last,
-    ) = refs[40:]
+    ) = refs[2 * N_IN + 2 :]
     (
         pressure,
         geo_diag,
@@ -189,9 +208,7 @@
         third,
         third_t,
         gather,
-        scatter,
-        pick_p,
-        pick_q,
+        pick,
         cols_first,
         cols_second,
     ) = vmem
@@ -231,9 +248,9 @@
     count_c = at_c[-1].astype(jnp.int32) + at_c[1].astype(jnp.int32)
     neighbours = count_s + count_c + count_s * count_c
     loads = [
-        pltpu.make_async_copy(hbm[i], vmem[i], load_sem.at[i]) for i in range(19)
+        pltpu.make_async_copy(hbm[i], vmem[i], load_sem.at[i]) for i in range(N_IN)
     ]
-    order = [0, 9, 11, 1, 2, 10, 12, 3, 4, 5, 6, 7, 8, 13, 14, 15, 16, 17, 18]
+    order = [0, 9, 11, 1, 2, 10, 12, 5, 13, 3, 4, 14, 15, 16, 6, 7, 8]
     for i in order:
         loads[i].start()
 
@@ -243,20 +260,15 @@
 
     for i in (0, 9, 11):
         loads[i].wait()
-    pres = pressure[...].reshape(OWN, 128)
-    pres_split = split(pres)
-    left_split = split(left[...])
-    third_split = split(third[...])
+    pres = split(pressure[...].reshape(OWN, 128))
     per = N1 * N1
-    along = [
-        product(left_split, tuple(part[a * per : (a + 1) * per] for part in pres_split))
-        for a in range(AB)
-    ]
-    grad_third = product(pres_split, third_split)
+    along = []
+    for a in range(AB):
+        high, low = (part[a * per : (a + 1) * per] for part in pres)
+        along.append(dot(left[...], jnp.concatenate([high, low, high], axis=0)))
+    grad_third = lane_product(pres, third[...])
     for i in (1, 2, 10, 12):
         loads[i].wait()
-    left_t_split = split(left_t[...])
-    third_t_split = split(third_t[...])
     for a in range(AB):
         rows = pl.ds(a * N1, N1)
         d0, d1, d2 = (geo_diag[k, rows].reshape(per, 128) for k in range(3))
@@ -266,9 +278,11 @@
         flux_first = d0 * g1 + o0 * g2 + o1 * g3
         flux_second = o0 * g1 + d1 * g2 + o2 * g3
         flux_third = o1 * g1 + o2 * g2 + d2 * g3
-        both = split(jnp.concatenate([flux_first, flux_second], axis=0))
-        own[pl.ds(a * per, per), :] = product(left_t_split, both) + product(
-            split(flux_third), third_t_split
+        high, low = split(jnp.concatenate([flux_first, flux_second], axis=0))
+        own[pl.ds(a * per, per), :] = (
+            dot(left_t[...], jnp.concatenate([high, high], axis=0))
+            + dot(left_t[:, :128], low)
+            + lane_product(split(flux_third), third_t[...])
         )
     for k, node in enumerate((6, 7, 0, 1)):
         stage[pl.ds(k * NF, NF), :] = own[pl.ds(node, NF, stride=N1), :]
@@ -296,96 +310,95 @@
         )
     for_each(FAR_FIRST, -1, lambda slot: sends[slot].start())
 
-    for i in (3, 4, 5, 6, 7, 8, 13, 14, 15, 16, 17, 18):
+    for i in order[7:]:
         loads[i].wait()
     for m in range(M):
         modes3[m * 16 : m * 16 + CB, 0:M] = modes_third[m]
         modes12[m * 8 : m * 8 + AB, 0:M] = modes_first[m]
-        modes12[m * 8 + 3 : m * 8 + 4, 0:M] = modes_second[m]
-    eigen[0:AB, 0:M] = eigen_first[...]
-    eigen[8:9, 0:M] = eigen_second[...]
-    eigen[16 : 16 + CB, 0:M] = eigen_third[...]
-
-    spread = jnp.where(iota((128, WIDE), 0) == (iota((128, WIDE), 1) & 15), 1.0, 0.0).astype(F32)
-    diagonal = jnp.dot(modes3[...], spread, precision=HIGHEST, preferred_element_type=F32)
-    same = (iota((WIDE, WIDE), 0) & 15) == (iota((WIDE, WIDE), 1) >> 4)
-    diagonal = jnp.where(same, diagonal, 0.0)
-    fore = tuple(part.astype(BF16) for part in select(gather[...], diagonal))
+        modes12[m * 8 + 3 : m * 8 + 4, 64 : 64 + M] = modes_second[m]
+    for a in range(AB):
+        eigen[a : a + 1, 0:M] = eigen_first[a : a + 1, :]
+        eigen[a : a + 1, 64 : 64 + M] = eigen_second[...]
+    eigen[8 : 8 + CB, 0:M] = eigen_third[...]
+
+    spread = (iota((128, WIDE), 0) == (iota((128, WIDE), 1) & 15)).astype(F32).astype(BF16)
+    same = (iota((CB * M, WIDE), 0) & 15) == (iota((CB * M, WIDE), 1) >> 4)
+    fore = []
     back = []
-    for part in split(jnp.transpose(diagonal)):
-        back.append(dot(part, scatter[...]).astype(BF16))
-
-    take_p = pick_p[...].astype(F32)
-    take_q = pick_q[...].astype(F32)
-    nt = (((1,), (1,)), ((), ()))
-    by_p = lax.dot_general(take_p, modes12[...], nt, precision=HIGHEST, preferred_element_type=F32)
-    by_q = lax.dot_general(take_q, modes12[...], nt, precision=HIGHEST, preferred_element_type=F32)
-    by_p = jnp.where(block_of(iota((ROWS, 128), 0)) == (iota((ROWS, 128), 1) & 7), by_p, 0.0)
-    by_p_split, by_q_split = split(by_p), split(by_q)
-    forward = (dot(by_p_split[0], cols_first[...]) + dot(by_p_split[1], cols_first[...])) * (
-        dot(by_q_split[0], cols_second[...]) + dot(by_q_split[1], cols_second[...])
-    )
-    forward_own = forward[:, :OWN]
-    forward_halo = forward[:, OWN:]
-    own_split = split(forward_own)
-    halo_split = split(forward_halo)
+    node, box = iota((128, WIDE), 0), iota((128, WIDE), 1) >> 4
+    stays = jnp.logical_or(
+        (node >> 3) == box, jnp.logical_or((node & 7) == 0, (node & 7) == 7)
+    )
+    for part in split(modes3[...]):
+        diagonal = jnp.where(same, dot(part, spread), 0.0).astype(BF16)
+        moved = dot(gather[...], diagonal)
+        fore.append(moved.astype(BF16))
+        back.append(jnp.where(stays, moved, 0.0).astype(BF16))
+
+    both = jnp.concatenate(split(modes12[...]), axis=0)
+    picked = lax.dot_general(
+        pick[...], both, (((1,), (1,)), ((), ())), preferred_element_type=F32
+    )
+    at_block = block_of(iota((ROWS, WIDE), 0)) == (iota((ROWS, WIDE), 1) & 7)
+    by_p = jnp.where(at_block, picked, 0.0).astype(BF16)
+    by_q = picked.astype(BF16)
+    forward = dot(by_p, jnp.concatenate([cols_first[...]] * 2, axis=0)) * dot(
+        by_q, jnp.concatenate([cols_second[...]] * 2, axis=0)
+    )
+    own_split = split(forward[:, :OWN])
+    halo_split = split(forward[:, OWN:])
 
     relative = (iota((ROWS, WIDE), 1) >> 3) + 2 - N1 * block_of(iota((ROWS, WIDE), 0))
     keep = jnp.logical_and(relative != 0, relative != 11)
     square = jnp.where(keep, forward[:, :WIDE], 0.0)
     square = jnp.concatenate([square, jnp.zeros((DEEP - ROWS, WIDE), F32)], axis=0)
-    kept[...] = jnp.transpose(square)
-    back_own = split(kept[pl.ds(0, OWN), :])
+    turned = jnp.transpose(square)
+    for k in range(3):
+        kept[k] = turned[:, k * 128 : (k + 1) * 128]
+
+    def kept_rows(rows):
+        return jnp.concatenate([kept[k, rows, :] for k in range(3)], axis=1)
+
+    back_own = split(kept_rows(pl.ds(0, OWN)))
     back_edge = split(
         jnp.concatenate(
             [
-                kept[pl.ds(0, 8), :],
-                kept[pl.ds(OWN - 8, 8), :],
+                kept_rows(pl.ds(7, NF, stride=N1)),
+                kept_rows(pl.ds(0, NF, stride=N1)),
+                kept_rows(pl.ds(OWN - 8, 8)),
+                kept_rows(pl.ds(0, 8)),
             ],
             axis=0,
         )
     )
-    back_far = split(
-        jnp.concatenate(
-            [kept[pl.ds(7 + 8 * f, 1), :] for f in range(NF)]
-            + [kept[pl.ds(8 * f, 1), :] for f in range(NF)],
-            axis=0,
-        )
-    )
-
-    third_eigen = jnp.dot(
-        eigen[16 : 16 + CB, :], spread, precision=HIGHEST, preferred_element_type=F32
-    )
-    third_eigen = jnp.where(
-        iota((CB, WIDE), 0) == (iota((CB, WIDE), 1) >> 4), third_eigen, 0.0
-    )
-    lane_part = jnp.sum(third_eigen, axis=0, keepdims=True)
+
+    third_eigen = eigen[8 : 8 + CB, :]
+    for shift in (16, 32, 64):
+        third_eigen = third_eigen + pltpu.roll(third_eigen, shift, 1)
+    third_eigen = jnp.concatenate([third_eigen, third_eigen], axis=1)
+    own_box = iota((CB, WIDE), 0) == (iota((CB, WIDE), 1) >> 4)
+    lane_part = jnp.sum(jnp.where(own_box, third_eigen, 0.0), axis=0, keepdims=True)
     inverse = []
     edges = [0, STEP, 2 * STEP, ROWS]
     for a in range(AB):
         rows = slice(edges[a], edges[a + 1])
         row_part = jnp.sum(
-            take_p[rows] * eigen[a : a + 1, :] + take_q[rows] * eigen[8:9, :],
-            axis=1,
-            keepdims=True,
+            pick[...].astype(F32)[rows] * eigen[a : a + 1, :], axis=1, keepdims=True
         )
         total = row_part + lane_part
         inverse.append(1.0 / jnp.where(total > 0.0, total, 1.0))
     inverse = jnp.concatenate(inverse, axis=0)
 
-    own_third = product(split(own[...]), fore)
+    own_third = wide_product(split(own[...]), fore)
     spectral_own = product(own_split, split(own_third))
 
     for_each(range(8), 1, lambda slot: sends[slot].wait_recv())
-    halo_third = product(split(halo[...]), fore)
+    halo_third = wide_product(split(halo[...]), fore)
     spectral = (spectral_own + product(halo_split, split(halo_third))) * inverse
     spectral = split(
         jnp.concatenate([spectral, jnp.zeros((DEEP - ROWS, WIDE), F32)], axis=0)
     )
-    stage_last[pl.ds(0, 48), :] = product(split(product(back_far, spectral)), back)
-    edge = product(split(product(back_edge, spectral)), back)
-    stage_last[pl.ds(48, 8), :] = edge[8:16]
-    stage_last[pl.ds(56, 8), :] = edge[0:8]
+    stage_last[...] = product_nt(split(product(back_edge, spectral)), back)
     last = {}
     for slot, (side_s, side_c) in enumerate(SLOTS):
         last[slot] = pltpu.make_async_remote_copy(
@@ -430,7 +443,7 @@
     )
     op_ref[...] = (value + from_left + from_right).reshape(NF, N1, 128)
 
-    solved[...] = product(split(product(back_own, spectral)), back)
+    solved[...] = product_nt(split(product(back_own, spectral)), back)
 
     for_each(range(8), 1, lambda slot: last[slot].wait_recv())
     for node, row in ((0, 0), (7, 24)):
@@ -450,12 +463,23 @@
     for_each(range(8), -1, lambda slot: last[slot].wait_send())
 
 
+def write_out(op_in, pre_in, op_out, pre_out, sem):
+    copies = [
+        pltpu.make_async_copy(source, target, sem.at[i])
+        for i, (source, target) in enumerate(((op_in, op_out), (pre_in, pre_out)))
+    ]
+    for copy in copies:
+        copy.start()
+    for copy in copies:
+        copy.wait()
+
+
 def shards(*args):
     operands = list(args) + [jnp.asarray(t) for t in tables()]
     for i in (3, 4, 5):
         operands[i] = jnp.transpose(operands[i], (1, 0, 2))
-    out = jax.ShapeDtypeStruct((NF, N1, CB * N1), F32)
-    return pl.pallas_call(
+    out = pltpu.VMEM((NF, N1, CB * N1), F32)
+    held = pl.pallas_call(
         kernel,
         out_shape=(out, out),
         in_specs=[pl.BlockSpec(memory_space=pl.ANY)] * len(operands),
@@ -469,11 +493,11 @@
             pltpu.VMEM((96, 128), F32),
             pltpu.VMEM((OWN, 128), F32),
             pltpu.VMEM((OWN, 128), F32),
-            pltpu.VMEM((WIDE, DEEP), F32),
-            pltpu.VMEM((WIDE, 128), F32),
+            pltpu.VMEM((3, WIDE, 128), F32),
+            pltpu.VMEM((CB * M, 128), F32),
             pltpu.VMEM((128, 128), F32),
             pltpu.VMEM((32, 128), F32),
-            pltpu.SemaphoreType.DMA((19,)),
+            pltpu.SemaphoreType.DMA((N_IN,)),
             pltpu.SemaphoreType.DMA((8,)),
             pltpu.SemaphoreType.DMA((8,)),
             pltpu.SemaphoreType.DMA((8,)),
@@ -482,6 +506,16 @@
         compiler_params=pltpu.CompilerParams(collective_id=0, has_side_effects=True),
         name="pressure_step",
     )(*operands)
+    held = [pltpu.with_memory_space_constraint(value, pltpu.VMEM) for value in held]
+    out = jax.ShapeDtypeStruct((NF, N1, CB * N1), F32)
+    return pl.pallas_call(
+        write_out,
+        out_shape=(out, out),
+        in_specs=[pl.BlockSpec(memory_space=pltpu.VMEM)] * 2,
+        out_specs=(pl.BlockSpec(memory_space=pl.ANY),) * 2,
+        scratch_shapes=[pltpu.SemaphoreType.DMA((2,))],
+        name="write_out",
+    )(*held)
 
 
 def solution(mesh):

time: 37.4 us -> 35.1 us (0.939)
  the two profiles are of different devices: /device:TPU:41 before, /device:TPU:47 now
where the time goes in v3:
time: 35.1 us; the launch traced here: 34.7 us
  Pallas kernels  34 us (97%)
  between operations  0.64 us (2%)
    pallas_call x1, Pallas kernels, shards(): pl.pallas_call(kernel, out_shape=(out, out), in_specs=[pl.BlockSpec(memor...  33.3 us

profile of v3, /device:TPU:47, one launch (start us, length us, event | category | flops | bytes accessed | tf_op | source)
XLA Modules:
  0.0 34.7 jit_solution(8021653380262865500)
XLA Ops:
  0.6 33.3 %pressure_step.1 = (f32[24,8,128]{2,1,0:T(8,128)S(1)}, f32[24,8,128]{2,1,0:T(8,128)S(1)}) custom-call(f32[24,8,128]{2,1,0:T(8,128)} %refs_0_.1, f32[3,24,8,128]{3,2,1,0:T(8,128)} %refs_1_.1, f32[3,24,8,128]{3,2,1,0:T(8,128)} %refs_2_.1, f32[10,3,10]{2,1,0:T(4,128)} %bitcast.4, f32[10,1,10]{2,1,0:T(1,128)} %bitcast.5, f32[10,16,10]{2,1,0:T(8,128)} %bitcast.3, ...), custom_call_target="tpu_custom_call" | custom-call | tf_op jit(solution)/shard_map/pressure_step/pallas_call | solution.py:482
  34.0 0.7 %write_out.1 = (f32[24,8,128]{2,1,0:T(8,128)}, f32[24,8,128]{2,1,0:T(8,128)}) custom-call(f32[24,8,128]{2,1,0:T(8,128)S(1)} %get-tuple-element.4.op_in, f32[24,8,128]{2,1,0:T(8,128)S(1)} %get-tuple-element.5.pre_in), custom_call_target="tpu_custom_call" | custom-call | tf_op jit(solution)/shard_map/write_out/pallas_call | solution.py:511

commit v4 on v3

--- a/solution.py
+++ b/solution.py
@@ -24,9 +24,12 @@
 BF16 = jnp.bfloat16
 MESH = pl.DeviceIdType.MESH
 N_IN = 17
+RUN = 8
+BEHIND = (1, 5, 7)
+RELAY_LEN = 80
 
 SLOTS = ((0, -1), (0, 1), (-1, 0), (1, 0), (-1, -1), (-1, 1), (1, -1), (1, 1))
-FIRST_AT = (0, 48, 96, 112, 128, 144, 160, 176)
+FIRST_AT = (0, 48, 128, 144, 160, 96, 176, 112)
 FIRST_LEN = (48, 48, 16, 16, 16, 16, 16, 16)
 LAST_AT = (0, 24, 48, 56, 64, 72, 80, 88)
 LAST_LEN = (24, 24, 8, 8, 8, 8, 8, 8)
@@ -192,6 +195,9 @@
         recv_sem,
         send_last,
         recv_last,
+        relay,
+        relay_sem,
+        forward_sem,
     ) = refs[2 * N_IN + 2 :]
     (
         pressure,
@@ -224,6 +230,13 @@
     at_s = {-1: me_s > 0, 0: True, 1: me_s < n_s - 1}
     at_c = {-1: me_c > 0, 0: True, 1: me_c < n_c - 1}
 
+    is_last = jnp.logical_and(lax.rem(me_c, RUN) == RUN - 1, me_c < n_c - 1)
+    is_start = jnp.logical_and(lax.rem(me_c, RUN) == 0, me_c > 0)
+    is_relay = jnp.logical_and(lax.rem(me_c, RUN) == 1, me_c + RUN - 1 < n_c)
+
+    def both(first, second):
+        return second if first is True else jnp.logical_and(first, second)
+
     def there(side_s, side_c):
         if side_s == 0:
             return at_c[side_c]
@@ -236,17 +249,32 @@
             side_s, side_c = SLOTS[slot]
             pl.when(there(sign * side_s, sign * side_c))(functools.partial(act, slot))
 
+    def to_relay(act):
+        for slot in BEHIND:
+            pl.when(both(at_s[-SLOTS[slot][0]], is_start))(functools.partial(act, slot))
+
+    def at_relay(act):
+        for slot in BEHIND:
+            pl.when(both(at_s[SLOTS[slot][0]], is_relay))(functools.partial(act, slot))
+
     halo[...] = jnp.zeros_like(halo)
     halo_last[...] = jnp.zeros_like(halo_last)
+    relay[...] = jnp.zeros_like(relay)
     barrier = pltpu.get_barrier_semaphore()
 
-    def greet(slot):
-        pl.semaphore_signal(barrier, inc=1, device_id=peer(*SLOTS[slot]), device_id_type=MESH)
-
-    for_each(range(8), 1, greet)
+    def greet(side_s, side_c):
+        pl.semaphore_signal(barrier, inc=1, device_id=peer(side_s, side_c), device_id_type=MESH)
+
+    pl.when(is_last)(functools.partial(greet, 0, 2 - RUN))
+    for side_s, side_c in SLOTS:
+        here = there(side_s, side_c)
+        if side_c > 0:
+            here = jnp.logical_and(here, jnp.logical_not(is_last))
+        pl.when(here)(functools.partial(greet, side_s, side_c))
+    at_relay(lambda slot: greet(SLOTS[slot][0], RUN - 1))
     count_s = at_s[-1].astype(jnp.int32) + at_s[1].astype(jnp.int32)
     count_c = at_c[-1].astype(jnp.int32) + at_c[1].astype(jnp.int32)
-    neighbours = count_s + count_c + count_s * count_c
+    neighbours = count_s + count_c + count_s * count_c + is_relay.astype(jnp.int32)
     loads = [
         pltpu.make_async_copy(hbm[i], vmem[i], load_sem.at[i]) for i in range(N_IN)
     ]
@@ -308,7 +336,33 @@
             device_id=peer(-side_s, -side_c),
             device_id_type=MESH,
         )
-    for_each(FAR_FIRST, -1, lambda slot: sends[slot].start())
+    relayed = {}
+    for slot in BEHIND:
+        relayed[slot] = pltpu.make_async_remote_copy(
+            src_ref=first_from[slot],
+            dst_ref=relay.at[pl.ds(FIRST_AT[slot] - 48, FIRST_LEN[slot]), :],
+            send_sem=send_sem.at[slot],
+            recv_sem=relay_sem.at[BEHIND.index(slot)],
+            device_id=peer(-SLOTS[slot][0], 1 - RUN),
+            device_id_type=MESH,
+        )
+    handed = pltpu.make_async_remote_copy(
+        src_ref=relay,
+        dst_ref=halo.at[pl.ds(48, RELAY_LEN), :],
+        send_sem=forward_sem.at[0],
+        recv_sem=forward_sem.at[1],
+        device_id=peer(0, RUN - 2),
+        device_id_type=MESH,
+    )
+    at_relay(lambda slot: relayed[slot].wait_recv())
+    pl.when(is_relay)(handed.start)
+    for slot in FAR_FIRST:
+        side_s, side_c = SLOTS[slot]
+        here = there(-side_s, -side_c)
+        if slot in BEHIND:
+            here = jnp.logical_and(here, jnp.logical_not(is_start))
+        pl.when(here)(sends[slot].start)
+    to_relay(lambda slot: relayed[slot].start())
 
     for i in order[7:]:
         loads[i].wait()
@@ -335,9 +389,9 @@
         fore.append(moved.astype(BF16))
         back.append(jnp.where(stays, moved, 0.0).astype(BF16))
 
-    both = jnp.concatenate(split(modes12[...]), axis=0)
+    modes_parts = jnp.concatenate(split(modes12[...]), axis=0)
     picked = lax.dot_general(
-        pick[...], both, (((1,), (1,)), ((), ())), preferred_element_type=F32
+        pick[...], modes_parts, (((1,), (1,)), ((), ())), preferred_element_type=F32
     )
     at_block = block_of(iota((ROWS, WIDE), 0)) == (iota((ROWS, WIDE), 1) & 7)
     by_p = jnp.where(at_block, picked, 0.0).astype(BF16)
@@ -392,7 +446,12 @@
     own_third = wide_product(split(own[...]), fore)
     spectral_own = product(own_split, split(own_third))
 
-    for_each(range(8), 1, lambda slot: sends[slot].wait_recv())
+    for slot in range(8):
+        here = there(*SLOTS[slot])
+        if slot in BEHIND:
+            here = jnp.logical_and(here, jnp.logical_not(is_last))
+        pl.when(here)(sends[slot].wait_recv)
+    pl.when(is_last)(handed.wait_recv)
     halo_third = wide_product(split(halo[...]), fore)
     spectral = (spectral_own + product(halo_split, split(halo_third))) * inverse
     spectral = split(
@@ -461,6 +520,7 @@
 
     for_each(range(8), -1, lambda slot: sends[slot].wait_send())
     for_each(range(8), -1, lambda slot: last[slot].wait_send())
+    pl.when(is_relay)(handed.wait_send)
 
 
 def write_out(op_in, pre_in, op_out, pre_out, sem):
@@ -502,6 +562,9 @@
             pltpu.SemaphoreType.DMA((8,)),
             pltpu.SemaphoreType.DMA((8,)),
             pltpu.SemaphoreType.DMA((8,)),
+            pltpu.VMEM((RELAY_LEN, 128), F32),
+            pltpu.SemaphoreType.DMA((3,)),
+            pltpu.SemaphoreType.DMA((2,)),
         ],
         compiler_params=pltpu.CompilerParams(collective_id=0, has_side_effects=True),
         name="pressure_step",

time: 35.1 us -> 31.8 us (0.906)
  Pallas kernels: 34 us -> 31 us
    pallas_call x1, Pallas kernels: 33.3 us -> 30.3 us  [shards(): pl.pallas_call(kernel, out_shape=(out, out), in_specs=[pl.BlockSpec(memor...]
where the time goes in v4:
time: 31.8 us; the launch traced here: 31.6 us
  Pallas kernels  31 us (97%)
  between operations  0.64 us (2%)
    pallas_call x1, Pallas kernels, shards(): pl.pallas_call(kernel, out_shape=(out, out), in_specs=[pl.BlockSpec(memor...  30.3 us
    pallas_call x1, Pallas kernels, shards(): pl.pallas_call(write_out, out_shape=(out, out), in_specs=[pl.BlockSpec(me...  0.69 us

profile of v4, /device:TPU:47, one launch (start us, length us, event | category | flops | bytes accessed | tf_op | source)
XLA Modules:
  0.0 31.6 jit_solution(3435027909201782412)
XLA Ops:
  0.6 30.3 %pressure_step.1 = (f32[24,8,128]{2,1,0:T(8,128)S(1)}, f32[24,8,128]{2,1,0:T(8,128)S(1)}) custom-call(f32[24,8,128]{2,1,0:T(8,128)} %refs_0_.1, f32[3,24,8,128]{3,2,1,0:T(8,128)} %refs_1_.1, f32[3,24,8,128]{3,2,1,0:T(8,128)} %refs_2_.1, f32[10,3,10]{2,1,0:T(4,128)} %bitcast.4, f32[10,1,10]{2,1,0:T(1,128)} %bitcast.5, f32[10,16,10]{2,1,0:T(8,128)} %bitcast.3, ...), custom_call_target="tpu_custom_call" | custom-call | tf_op jit(solution)/shard_map/pressure_step/pallas_call | solution.py:542
  30.9 0.7 %write_out.1 = (f32[24,8,128]{2,1,0:T(8,128)}, f32[24,8,128]{2,1,0:T(8,128)}) custom-call(f32[24,8,128]{2,1,0:T(8,128)S(1)} %get-tuple-element.4.op_in, f32[24,8,128]{2,1,0:T(8,128)S(1)} %get-tuple-element.5.pre_in), custom_call_target="tpu_custom_call" | custom-call | tf_op jit(solution)/shard_map/write_out/pallas_call | solution.py:574

commit v5 on v4

--- a/solution.py
+++ b/solution.py
@@ -198,6 +198,7 @@
         relay,
         relay_sem,
         forward_sem,
+        ready_sem,
     ) = refs[2 * N_IN + 2 :]
     (
         pressure,
@@ -234,9 +235,6 @@
     is_start = jnp.logical_and(lax.rem(me_c, RUN) == 0, me_c > 0)
     is_relay = jnp.logical_and(lax.rem(me_c, RUN) == 1, me_c + RUN - 1 < n_c)
 
-    def both(first, second):
-        return second if first is True else jnp.logical_and(first, second)
-
     def there(side_s, side_c):
         if side_s == 0:
             return at_c[side_c]
@@ -244,18 +242,19 @@
             return at_s[side_s]
         return jnp.logical_and(at_s[side_s], at_c[side_c])
 
+    def both(first, second):
+        return second if first is True else jnp.logical_and(first, second)
+
+    def when(act, *conditions):
+        pl.when(functools.reduce(both, conditions, True))(act)
+
     def for_each(order, sign, act):
         for slot in order:
             side_s, side_c = SLOTS[slot]
-            pl.when(there(sign * side_s, sign * side_c))(functools.partial(act, slot))
-
-    def to_relay(act):
-        for slot in BEHIND:
-            pl.when(both(at_s[-SLOTS[slot][0]], is_start))(functools.partial(act, slot))
-
-    def at_relay(act):
-        for slot in BEHIND:
-            pl.when(both(at_s[SLOTS[slot][0]], is_relay))(functools.partial(act, slot))
+            when(functools.partial(act, slot), there(sign * side_s, sign * side_c))
+
+    not_last = jnp.logical_not(is_last)
+    not_start = jnp.logical_not(is_start)
 
     halo[...] = jnp.zeros_like(halo)
     halo_last[...] = jnp.zeros_like(halo_last)
@@ -265,16 +264,23 @@
     def greet(side_s, side_c):
         pl.semaphore_signal(barrier, inc=1, device_id=peer(side_s, side_c), device_id_type=MESH)
 
-    pl.when(is_last)(functools.partial(greet, 0, 2 - RUN))
-    for side_s, side_c in SLOTS:
-        here = there(side_s, side_c)
-        if side_c > 0:
-            here = jnp.logical_and(here, jnp.logical_not(is_last))
-        pl.when(here)(functools.partial(greet, side_s, side_c))
-    at_relay(lambda slot: greet(SLOTS[slot][0], RUN - 1))
+    def hello(side_s, side_c, *conditions):
+        when(functools.partial(greet, side_s, side_c), at_s[side_s], *conditions)
+
+    hello(0, 2 - RUN, is_last)
+    hello(-1, 0)
+    hello(1, 0)
+    hello(0, 1, at_c[1], not_last)
+    for side_s in (0, -1, 1):
+        hello(side_s, -1, is_start)
+        hello(side_s, RUN - 1, is_relay)
     count_s = at_s[-1].astype(jnp.int32) + at_s[1].astype(jnp.int32)
-    count_c = at_c[-1].astype(jnp.int32) + at_c[1].astype(jnp.int32)
-    neighbours = count_s + count_c + count_s * count_c + is_relay.astype(jnp.int32)
+    neighbours = (
+        count_s
+        + jnp.logical_and(at_c[-1], not_start).astype(jnp.int32)
+        + (1 + count_s) * jnp.logical_or(is_last, is_start).astype(jnp.int32)
+        + is_relay.astype(jnp.int32)
+    )
     loads = [
         pltpu.make_async_copy(hbm[i], vmem[i], load_sem.at[i]) for i in range(N_IN)
     ]
@@ -354,15 +360,49 @@
         device_id=peer(0, RUN - 2),
         device_id_type=MESH,
     )
-    at_relay(lambda slot: relayed[slot].wait_recv())
-    pl.when(is_relay)(handed.start)
-    for slot in FAR_FIRST:
+    onward = {}
+    for slot in (4, 5, 6, 7):
         side_s, side_c = SLOTS[slot]
-        here = there(-side_s, -side_c)
-        if slot in BEHIND:
-            here = jnp.logical_and(here, jnp.logical_not(is_start))
-        pl.when(here)(sends[slot].start)
-    to_relay(lambda slot: relayed[slot].start())
+        onward[slot] = pltpu.make_async_remote_copy(
+            src_ref=halo.at[pl.ds(FIRST_AT[2 if side_s < 0 else 3], 16), :],
+            dst_ref=halo.at[pl.ds(FIRST_AT[slot], 16), :],
+            send_sem=send_sem.at[slot],
+            recv_sem=recv_sem.at[slot],
+            device_id=peer(0, -side_c),
+            device_id_type=MESH,
+        )
+    for slot in BEHIND:
+        when(relayed[slot].wait_recv, is_relay, at_s[SLOTS[slot][0]])
+    when(handed.start, is_relay)
+
+    def say_ready():
+        pl.semaphore_signal(ready_sem, inc=1, device_id=peer(0, -1), device_id_type=MESH)
+
+    def hear_ready():
+        pl.semaphore_wait(ready_sem, 1)
+
+    when(say_ready, at_c[-1], not_start)
+    when(sends[2].start, at_s[1])
+    when(sends[3].start, at_s[-1])
+    when(sends[1].start, at_c[-1], not_start)
+    for slot in (4, 6, 0):
+        when(sends[slot].start, is_last, at_s[-SLOTS[slot][0]])
+    for slot in BEHIND:
+        when(relayed[slot].start, is_start, at_s[-SLOTS[slot][0]])
+    when(hear_ready, at_c[1], not_last)
+    when(sends[0].start, at_c[1], not_last)
+
+    def hand_on(turn):
+        for source in (2, 3):
+            side = SLOTS[source][0]
+            when(sends[source].wait_recv, turn, at_s[side])
+            for slot in (4, 5, 6, 7):
+                side_s, side_c = SLOTS[slot]
+                if side_s == side:
+                    allowed = not_last if side_c < 0 else not_start
+                    when(onward[slot].start, turn, at_s[side], at_c[-side_c], allowed)
+
+    hand_on(not_last)
 
     for i in order[7:]:
         loads[i].wait()
@@ -446,11 +486,10 @@
     own_third = wide_product(split(own[...]), fore)
     spectral_own = product(own_split, split(own_third))
 
-    for slot in range(8):
-        here = there(*SLOTS[slot])
-        if slot in BEHIND:
-            here = jnp.logical_and(here, jnp.logical_not(is_last))
-        pl.when(here)(sends[slot].wait_recv)
+    hand_on(is_last)
+    for slot in (0, 1, 4, 5, 6, 7):
+        arrives = not_last if slot in BEHIND else True
+        when(sends[slot].wait_recv, there(*SLOTS[slot]), arrives)
     pl.when(is_last)(handed.wait_recv)
     halo_third = wide_product(split(halo[...]), fore)
     spectral = (spectral_own + product(halo_split, split(halo_third))) * inverse
@@ -518,7 +557,13 @@
     solved[pl.ds(OWN - 8, 8), :] = solved[pl.ds(OWN - 8, 8), :] + layer_last(3, 6, 7)
     pre_ref[...] = solved[...].reshape(NF, N1, 128)
 
-    for_each(range(8), -1, lambda slot: sends[slot].wait_send())
+    for_each(range(4), -1, lambda slot: sends[slot].wait_send())
+    for slot in (4, 5, 6, 7):
+        side_s, side_c = SLOTS[slot]
+        direct = is_last if side_c < 0 else is_start
+        straight = both(at_s[-side_s], direct)
+        passed = both(at_s[side_s], jnp.logical_and(at_c[-side_c], jnp.logical_not(direct)))
+        when(sends[slot].wait_send, jnp.logical_or(straight, passed))
     for_each(range(8), -1, lambda slot: last[slot].wait_send())
     pl.when(is_relay)(handed.wait_send)
 
@@ -565,6 +610,7 @@
             pltpu.VMEM((RELAY_LEN, 128), F32),
             pltpu.SemaphoreType.DMA((3,)),
             pltpu.SemaphoreType.DMA((2,)),
+            pltpu.SemaphoreType.REGULAR,
         ],
         compiler_params=pltpu.CompilerParams(collective_id=0, has_side_effects=True),
         name="pressure_step",

time: 31.8 us -> 32.3 us (1.016)
  Pallas kernels: 31 us -> 31.4 us
    pallas_call x1, Pallas kernels: 30.3 us -> 30.7 us  [shards(): pl.pallas_call(kernel, out_shape=(out, out), in_specs=[pl.BlockSpec(memor...]
where the time goes in v5:
time: 32.3 us; the launch traced here: 32.1 us
  Pallas kernels  31.4 us (97%)
  between operations  0.64 us (2%)
    pallas_call x1, Pallas kernels, shards(): pl.pallas_call(kernel, out_shape=(out, out), in_specs=[pl.BlockSpec(memor...  30.7 us
    pallas_call x1, Pallas kernels, shards(): pl.pallas_call(write_out, out_shape=(out, out), in_specs=[pl.BlockSpec(me...  0.69 us

profile of v5, /device:TPU:47, one launch (start us, length us, event | category | flops | bytes accessed | tf_op | source)
XLA Modules:
  0.0 32.1 jit_solution(4315821198246158050)
XLA Ops:
  0.6 30.7 %pressure_step.1 = (f32[24,8,128]{2,1,0:T(8,128)S(1)}, f32[24,8,128]{2,1,0:T(8,128)S(1)}) custom-call(f32[24,8,128]{2,1,0:T(8,128)} %refs_0_.1, f32[3,24,8,128]{3,2,1,0:T(8,128)} %refs_1_.1, f32[3,24,8,128]{3,2,1,0:T(8,128)} %refs_2_.1, f32[10,3,10]{2,1,0:T(4,128)} %bitcast.4, f32[10,1,10]{2,1,0:T(1,128)} %bitcast.5, f32[10,16,10]{2,1,0:T(8,128)} %bitcast.3, ...), custom_call_target="tpu_custom_call" | custom-call | tf_op jit(solution)/shard_map/pressure_step/pallas_call | solution.py:587
  31.4 0.7 %write_out.1 = (f32[24,8,128]{2,1,0:T(8,128)}, f32[24,8,128]{2,1,0:T(8,128)}) custom-call(f32[24,8,128]{2,1,0:T(8,128)S(1)} %get-tuple-element.4.op_in, f32[24,8,128]{2,1,0:T(8,128)S(1)} %get-tuple-element.5.pre_in), custom_call_target="tpu_custom_call" | custom-call | tf_op jit(solution)/shard_map/write_out/pallas_call | solution.py:620

commit v6 on v5

--- a/solution.py
+++ b/solution.py
@@ -23,7 +23,7 @@
 F32 = jnp.float32
 BF16 = jnp.bfloat16
 MESH = pl.DeviceIdType.MESH
-N_IN = 17
+N_IN = 11
 RUN = 8
 BEHIND = (1, 5, 7)
 RELAY_LEN = 80
@@ -134,7 +134,12 @@
         if second_layer[col] >= 0:
             cols_second[LAYER_NODE[second_layer[col]] * 8 + 3, col] = 1.0
     exact = [t.astype(BF16) for t in (gather, pick, cols_first, cols_second)]
-    return [left_all, left_t] + thirds + exact
+    left_all = np.concatenate([left_all, np.zeros((128, 64), BF16)], axis=1)
+    near = np.concatenate([left_all, left_t] + thirds, axis=0)
+    gather, pick, cols_first, cols_second = exact
+    gather = np.concatenate([gather, np.zeros((128, 96), BF16)], axis=1)
+    wide = [t[:, k : k + 128] for t in (gather, cols_first, cols_second) for k in range(0, t.shape[1], 128)]
+    return [near, np.concatenate([pick] + wide, axis=0)]
 
 
 def dot(a, b):
@@ -147,7 +152,9 @@
 
 
 def product(a, b):
-    return dot(a[0], b[0]) + (dot(a[1], b[0]) + dot(a[0], b[1]))
+    rows = a[0].shape[0]
+    both = dot(jnp.concatenate(a, axis=0), b[0])
+    return both[:rows] + (both[rows:] + dot(a[0], b[1]))
 
 
 def lane_product(a, table):
@@ -159,11 +166,14 @@
     return dot(jnp.concatenate(a, axis=1), jnp.concatenate([b[0], b[0]], axis=0)) + dot(a[0], b[1])
 
 
+def dot_nt(a, b):
+    return lax.dot_general(a, b, (((1,), (1,)), ((), ())), preferred_element_type=F32)
+
+
 def product_nt(a, b):
-    def one(x, y):
-        return lax.dot_general(x, y, (((1,), (1,)), ((), ())), preferred_element_type=F32)
-
-    return one(a[0], b[0]) + (one(a[1], b[0]) + one(a[0], b[1]))
+    rows = a[0].shape[0]
+    both = dot_nt(jnp.concatenate(a, axis=0), b[0])
+    return both[:rows] + (both[rows:] + dot_nt(a[0], b[1]))
 
 
 def iota(shape, dimension):
@@ -193,7 +203,6 @@
         load_sem,
         send_sem,
         recv_sem,
-        send_last,
         recv_last,
         relay,
         relay_sem,
@@ -210,15 +219,17 @@
         eigen_first,
         eigen_second,
         eigen_third,
-        left,
-        left_t,
-        third,
-        third_t,
-        gather,
-        pick,
-        cols_first,
-        cols_second,
+        near,
+        far,
     ) = vmem
+    left, left_t = near.at[0:128, 0:192], near.at[128:192, :]
+    third, third_t = near.at[192:448, :], near.at[448:704, :]
+    pick = far.at[0:ROWS, :]
+
+    def table(first, count):
+        parts = [far[ROWS + 128 * k : ROWS + 128 * (k + 1), :] for k in range(first, first + count)]
+        return jnp.concatenate(parts, axis=1)
+
     n_s, n_c = lax.axis_size("stream"), lax.axis_size("cross")
     me_s, me_c = lax.axis_index("stream"), lax.axis_index("cross")
 
@@ -284,7 +295,7 @@
     loads = [
         pltpu.make_async_copy(hbm[i], vmem[i], load_sem.at[i]) for i in range(N_IN)
     ]
-    order = [0, 9, 11, 1, 2, 10, 12, 5, 13, 3, 4, 14, 15, 16, 6, 7, 8]
+    order = [0, 9, 1, 2, 5, 3, 4, 10, 6, 7, 8]
     for i in order:
         loads[i].start()
 
@@ -292,8 +303,17 @@
     modes12[...] = jnp.zeros_like(modes12)
     eigen[...] = jnp.zeros_like(eigen)
 
-    for i in (0, 9, 11):
-        loads[i].wait()
+    loads[0].wait()
+
+    def say_ready():
+        pl.semaphore_signal(ready_sem, inc=1, device_id=peer(0, -1), device_id_type=MESH)
+
+    def hear_ready():
+        pl.semaphore_wait(ready_sem, 1)
+
+    pl.semaphore_wait(barrier, neighbours)
+    when(say_ready, at_c[-1], not_start)
+    loads[9].wait()
     pres = split(pressure[...].reshape(OWN, 128))
     per = N1 * N1
     along = []
@@ -301,7 +321,7 @@
         high, low = (part[a * per : (a + 1) * per] for part in pres)
         along.append(dot(left[...], jnp.concatenate([high, low, high], axis=0)))
     grad_third = lane_product(pres, third[...])
-    for i in (1, 2, 10, 12):
+    for i in (1, 2):
         loads[i].wait()
     for a in range(AB):
         rows = pl.ds(a * N1, N1)
@@ -321,7 +341,6 @@
     for k, node in enumerate((6, 7, 0, 1)):
         stage[pl.ds(k * NF, NF), :] = own[pl.ds(node, NF, stride=N1), :]
 
-    pl.semaphore_wait(barrier, neighbours)
     first_from = (
         stage.at[pl.ds(0, 48), :],
         stage.at[pl.ds(48, 48), :],
@@ -375,13 +394,6 @@
         when(relayed[slot].wait_recv, is_relay, at_s[SLOTS[slot][0]])
     when(handed.start, is_relay)
 
-    def say_ready():
-        pl.semaphore_signal(ready_sem, inc=1, device_id=peer(0, -1), device_id_type=MESH)
-
-    def hear_ready():
-        pl.semaphore_wait(ready_sem, 1)
-
-    when(say_ready, at_c[-1], not_start)
     when(sends[2].start, at_s[1])
     when(sends[3].start, at_s[-1])
     when(sends[1].start, at_c[-1], not_start)
@@ -404,7 +416,7 @@
 
     hand_on(not_last)
 
-    for i in order[7:]:
+    for i in order[4:]:
         loads[i].wait()
     for m in range(M):
         modes3[m * 16 : m * 16 + CB, 0:M] = modes_third[m]
@@ -425,7 +437,7 @@
     )
     for part in split(modes3[...]):
         diagonal = jnp.where(same, dot(part, spread), 0.0).astype(BF16)
-        moved = dot(gather[...], diagonal)
+        moved = dot(table(0, 2)[:, : CB * M], diagonal)
         fore.append(moved.astype(BF16))
         back.append(jnp.where(stays, moved, 0.0).astype(BF16))
 
@@ -436,8 +448,8 @@
     at_block = block_of(iota((ROWS, WIDE), 0)) == (iota((ROWS, WIDE), 1) & 7)
     by_p = jnp.where(at_block, picked, 0.0).astype(BF16)
     by_q = picked.astype(BF16)
-    forward = dot(by_p, jnp.concatenate([cols_first[...]] * 2, axis=0)) * dot(
-        by_q, jnp.concatenate([cols_second[...]] * 2, axis=0)
+    forward = dot(by_p, jnp.concatenate([table(2, 3)] * 2, axis=0)) * dot(
+        by_q, jnp.concatenate([table(5, 3)] * 2, axis=0)
     )
     own_split = split(forward[:, :OWN])
     halo_split = split(forward[:, OWN:])
@@ -487,6 +499,13 @@
     spectral_own = product(own_split, split(own_third))
 
     hand_on(is_last)
+    for_each(range(4), -1, lambda slot: sends[slot].wait_send())
+    for slot in (4, 5, 6, 7):
+        side_s, side_c = SLOTS[slot]
+        direct = is_last if side_c < 0 else is_start
+        straight = both(at_s[-side_s], direct)
+        passed = both(at_s[side_s], jnp.logical_and(at_c[-side_c], jnp.logical_not(direct)))
+        when(sends[slot].wait_send, jnp.logical_or(straight, passed))
     for slot in (0, 1, 4, 5, 6, 7):
         arrives = not_last if slot in BEHIND else True
         when(sends[slot].wait_recv, there(*SLOTS[slot]), arrives)
@@ -502,7 +521,7 @@
         last[slot] = pltpu.make_async_remote_copy(
             src_ref=stage_last.at[pl.ds(LAST_FROM[slot], LAST_LEN[slot]), :],
             dst_ref=halo_last.at[pl.ds(LAST_AT[slot], LAST_LEN[slot]), :],
-            send_sem=send_last.at[slot],
+            send_sem=send_sem.at[slot],
             recv_sem=recv_last.at[slot],
             device_id=peer(-side_s, -side_c),
             device_id_type=MESH,
@@ -557,13 +576,6 @@
     solved[pl.ds(OWN - 8, 8), :] = solved[pl.ds(OWN - 8, 8), :] + layer_last(3, 6, 7)
     pre_ref[...] = solved[...].reshape(NF, N1, 128)
 
-    for_each(range(4), -1, lambda slot: sends[slot].wait_send())
-    for slot in (4, 5, 6, 7):
-        side_s, side_c = SLOTS[slot]
-        direct = is_last if side_c < 0 else is_start
-        straight = both(at_s[-side_s], direct)
-        passed = both(at_s[side_s], jnp.logical_and(at_c[-side_c], jnp.logical_not(direct)))
-        when(sends[slot].wait_send, jnp.logical_or(straight, passed))
     for_each(range(8), -1, lambda slot: last[slot].wait_send())
     pl.when(is_relay)(handed.wait_send)
 
@@ -606,7 +618,6 @@
             pltpu.SemaphoreType.DMA((8,)),
             pltpu.SemaphoreType.DMA((8,)),
             pltpu.SemaphoreType.DMA((8,)),
-            pltpu.SemaphoreType.DMA((8,)),
             pltpu.VMEM((RELAY_LEN, 128), F32),
             pltpu.SemaphoreType.DMA((3,)),
             pltpu.SemaphoreType.DMA((2,)),

time: 32.3 us -> 32.7 us (1.012)
  the two profiles are of different devices: /device:TPU:47 before, /device:TPU:43 now
where the time goes in v6:
time: 32.7 us; the launch traced here: 32.5 us
  Pallas kernels  31.9 us (98%)
  between operations  0.64 us (2%)
    pallas_call x1, Pallas kernels, shards(): pl.pallas_call(kernel, out_shape=(out, out), in_specs=[pl.BlockSpec(memor...  31.2 us
    pallas_call x1, Pallas kernels, shards(): pl.pallas_call(write_out, out_shape=(out, out), in_specs=[pl.BlockSpec(me...  0.69 us

profile of v6, /device:TPU:43, one launch (start us, length us, event | category | flops | bytes accessed | tf_op | source)
XLA Modules:
  0.0 32.5 jit_solution(11942483838911497407)
XLA Ops:
  0.6 31.2 %pressure_step.1 = (f32[24,8,128]{2,1,0:T(8,128)S(1)}, f32[24,8,128]{2,1,0:T(8,128)S(1)}) custom-call(f32[24,8,128]{2,1,0:T(8,128)} %refs_0_.1, f32[3,24,8,128]{3,2,1,0:T(8,128)} %refs_1_.1, f32[3,24,8,128]{3,2,1,0:T(8,128)} %refs_2_.1, f32[10,3,10]{2,1,0:T(4,128)} %bitcast.4, f32[10,1,10]{2,1,0:T(1,128)} %bitcast.5, f32[10,16,10]{2,1,0:T(8,128)} %bitcast.3, ...), custom_call_target="tpu_custom_call" | custom-call | tf_op jit(solution)/shard_map/pressure_step/pallas_call | solution.py:599
  31.8 0.7 %write_out.1 = (f32[24,8,128]{2,1,0:T(8,128)}, f32[24,8,128]{2,1,0:T(8,128)}) custom-call(f32[24,8,128]{2,1,0:T(8,128)S(1)} %get-tuple-element.4.op_in, f32[24,8,128]{2,1,0:T(8,128)S(1)} %get-tuple-element.5.pre_in), custom_call_target="tpu_custom_call" | custom-call | tf_op jit(solution)/shard_map/write_out/pallas_call | solution.py:631

commit v7 on v6

--- a/solution.py
+++ b/solution.py
@@ -244,7 +244,7 @@
 
     is_last = jnp.logical_and(lax.rem(me_c, RUN) == RUN - 1, me_c < n_c - 1)
     is_start = jnp.logical_and(lax.rem(me_c, RUN) == 0, me_c > 0)
-    is_relay = jnp.logical_and(lax.rem(me_c, RUN) == 1, me_c + RUN - 1 < n_c)
+    is_relay = jnp.logical_and(lax.rem(me_c, RUN) == 0, me_c + RUN < n_c)
 
     def there(side_s, side_c):
         if side_s == 0:
@@ -278,19 +278,19 @@
     def hello(side_s, side_c, *conditions):
         when(functools.partial(greet, side_s, side_c), at_s[side_s], *conditions)
 
-    hello(0, 2 - RUN, is_last)
+    hello(0, RUN - 1, is_relay)
     hello(-1, 0)
     hello(1, 0)
     hello(0, 1, at_c[1], not_last)
     for side_s in (0, -1, 1):
         hello(side_s, -1, is_start)
-        hello(side_s, RUN - 1, is_relay)
+        hello(side_s, RUN, is_relay)
     count_s = at_s[-1].astype(jnp.int32) + at_s[1].astype(jnp.int32)
     neighbours = (
         count_s
         + jnp.logical_and(at_c[-1], not_start).astype(jnp.int32)
         + (1 + count_s) * jnp.logical_or(is_last, is_start).astype(jnp.int32)
-        + is_relay.astype(jnp.int32)
+        + is_last.astype(jnp.int32)
     )
     loads = [
         pltpu.make_async_copy(hbm[i], vmem[i], load_sem.at[i]) for i in range(N_IN)
@@ -305,14 +305,16 @@
 
     loads[0].wait()
 
-    def say_ready():
-        pl.semaphore_signal(ready_sem, inc=1, device_id=peer(0, -1), device_id_type=MESH)
-
-    def hear_ready():
-        pl.semaphore_wait(ready_sem, 1)
+    def say_ready(kind):
+        to = peer(0, (-1, 1 - RUN)[kind])
+        pl.semaphore_signal(ready_sem.at[kind], inc=1, device_id=to, device_id_type=MESH)
+
+    def hear_ready(kind):
+        pl.semaphore_wait(ready_sem.at[kind], 1)
 
     pl.semaphore_wait(barrier, neighbours)
-    when(say_ready, at_c[-1], not_start)
+    when(functools.partial(say_ready, 1), is_last)
+    when(functools.partial(say_ready, 0), at_c[-1], not_start)
     loads[9].wait()
     pres = split(pressure[...].reshape(OWN, 128))
     per = N1 * N1
@@ -368,7 +370,7 @@
             dst_ref=relay.at[pl.ds(FIRST_AT[slot] - 48, FIRST_LEN[slot]), :],
             send_sem=send_sem.at[slot],
             recv_sem=relay_sem.at[BEHIND.index(slot)],
-            device_id=peer(-SLOTS[slot][0], 1 - RUN),
+            device_id=peer(-SLOTS[slot][0], -RUN),
             device_id_type=MESH,
         )
     handed = pltpu.make_async_remote_copy(
@@ -376,7 +378,7 @@
         dst_ref=halo.at[pl.ds(48, RELAY_LEN), :],
         send_sem=forward_sem.at[0],
         recv_sem=forward_sem.at[1],
-        device_id=peer(0, RUN - 2),
+        device_id=peer(0, RUN - 1),
         device_id_type=MESH,
     )
     onward = {}
@@ -390,10 +392,6 @@
             device_id=peer(0, -side_c),
             device_id_type=MESH,
         )
-    for slot in BEHIND:
-        when(relayed[slot].wait_recv, is_relay, at_s[SLOTS[slot][0]])
-    when(handed.start, is_relay)
-
     when(sends[2].start, at_s[1])
     when(sends[3].start, at_s[-1])
     when(sends[1].start, at_c[-1], not_start)
@@ -401,7 +399,7 @@
         when(sends[slot].start, is_last, at_s[-SLOTS[slot][0]])
     for slot in BEHIND:
         when(relayed[slot].start, is_start, at_s[-SLOTS[slot][0]])
-    when(hear_ready, at_c[1], not_last)
+    when(functools.partial(hear_ready, 0), at_c[1], not_last)
     when(sends[0].start, at_c[1], not_last)
 
     def hand_on(turn):
@@ -415,6 +413,10 @@
                     when(onward[slot].start, turn, at_s[side], at_c[-side_c], allowed)
 
     hand_on(not_last)
+    for slot in BEHIND:
+        when(relayed[slot].wait_recv, is_relay, at_s[SLOTS[slot][0]])
+    when(functools.partial(hear_ready, 1), is_relay)
+    when(handed.start, is_relay)
 
     for i in order[4:]:
         loads[i].wait()
@@ -621,7 +623,7 @@
             pltpu.VMEM((RELAY_LEN, 128), F32),
             pltpu.SemaphoreType.DMA((3,)),
             pltpu.SemaphoreType.DMA((2,)),
-            pltpu.SemaphoreType.REGULAR,
+            pltpu.SemaphoreType.REGULAR((2,)),
         ],
         compiler_params=pltpu.CompilerParams(collective_id=0, has_side_effects=True),
         name="pressure_step",

time: 32.7 us -> 32.7 us (level)
  the two profiles are of different devices: /device:TPU:43 before, /device:TPU:47 now
where the time goes in v7:
time: 32.7 us; the launch traced here: 32.5 us
  Pallas kernels  31.8 us (97%)
  between operations  0.64 us (2%)
    pallas_call x1, Pallas kernels, shards(): pl.pallas_call(kernel, out_shape=(out, out), in_specs=[pl.BlockSpec(memor...  31.1 us
    pallas_call x1, Pallas kernels, shards(): pl.pallas_call(write_out, out_shape=(out, out), in_specs=[pl.BlockSpec(me...  0.69 us

profile of v7, /device:TPU:47, one launch (start us, length us, event | category | flops | bytes accessed | tf_op | source)
XLA Modules:
  0.0 32.5 jit_solution(5374669663654109018)
XLA Ops:
  0.6 31.1 %pressure_step.1 = (f32[24,8,128]{2,1,0:T(8,128)S(1)}, f32[24,8,128]{2,1,0:T(8,128)S(1)}) custom-call(f32[24,8,128]{2,1,0:T(8,128)} %refs_0_.1, f32[3,24,8,128]{3,2,1,0:T(8,128)} %refs_1_.1, f32[3,24,8,128]{3,2,1,0:T(8,128)} %refs_2_.1, f32[10,3,10]{2,1,0:T(4,128)} %bitcast.4, f32[10,1,10]{2,1,0:T(1,128)} %bitcast.5, f32[10,16,10]{2,1,0:T(8,128)} %bitcast.3, ...), custom_call_target="tpu_custom_call" | custom-call | tf_op jit(solution)/shard_map/pressure_step/pallas_call | solution.py:601
  31.8 0.7 %write_out.1 = (f32[24,8,128]{2,1,0:T(8,128)}, f32[24,8,128]{2,1,0:T(8,128)}) custom-call(f32[24,8,128]{2,1,0:T(8,128)S(1)} %get-tuple-element.4.op_in, f32[24,8,128]{2,1,0:T(8,128)S(1)} %get-tuple-element.5.pre_in), custom_call_target="tpu_custom_call" | custom-call | tf_op jit(solution)/shard_map/write_out/pallas_call | solution.py:633

commit v8 on v7

--- a/solution.py
+++ b/solution.py
@@ -203,6 +203,7 @@
         load_sem,
         send_sem,
         recv_sem,
+        send_last,
         recv_last,
         relay,
         relay_sem,
@@ -501,13 +502,6 @@
     spectral_own = product(own_split, split(own_third))
 
     hand_on(is_last)
-    for_each(range(4), -1, lambda slot: sends[slot].wait_send())
-    for slot in (4, 5, 6, 7):
-        side_s, side_c = SLOTS[slot]
-        direct = is_last if side_c < 0 else is_start
-        straight = both(at_s[-side_s], direct)
-        passed = both(at_s[side_s], jnp.logical_and(at_c[-side_c], jnp.logical_not(direct)))
-        when(sends[slot].wait_send, jnp.logical_or(straight, passed))
     for slot in (0, 1, 4, 5, 6, 7):
         arrives = not_last if slot in BEHIND else True
         when(sends[slot].wait_recv, there(*SLOTS[slot]), arrives)
@@ -523,7 +517,7 @@
         last[slot] = pltpu.make_async_remote_copy(
             src_ref=stage_last.at[pl.ds(LAST_FROM[slot], LAST_LEN[slot]), :],
             dst_ref=halo_last.at[pl.ds(LAST_AT[slot], LAST_LEN[slot]), :],
-            send_sem=send_sem.at[slot],
+            send_sem=send_last.at[slot],
             recv_sem=recv_last.at[slot],
             device_id=peer(-side_s, -side_c),
             device_id_type=MESH,
@@ -578,6 +572,13 @@
     solved[pl.ds(OWN - 8, 8), :] = solved[pl.ds(OWN - 8, 8), :] + layer_last(3, 6, 7)
     pre_ref[...] = solved[...].reshape(NF, N1, 128)
 
+    for_each(range(4), -1, lambda slot: sends[slot].wait_send())
+    for slot in (4, 5, 6, 7):
+        side_s, side_c = SLOTS[slot]
+        direct = is_last if side_c < 0 else is_start
+        straight = both(at_s[-side_s], direct)
+        passed = both(at_s[side_s], jnp.logical_and(at_c[-side_c], jnp.logical_not(direct)))
+        when(sends[slot].wait_send, jnp.logical_or(straight, passed))
     for_each(range(8), -1, lambda slot: last[slot].wait_send())
     pl.when(is_relay)(handed.wait_send)
 
@@ -620,6 +621,7 @@
             pltpu.SemaphoreType.DMA((8,)),
             pltpu.SemaphoreType.DMA((8,)),
             pltpu.SemaphoreType.DMA((8,)),
+            pltpu.SemaphoreType.DMA((8,)),
             pltpu.VMEM((RELAY_LEN, 128), F32),
             pltpu.SemaphoreType.DMA((3,)),
             pltpu.SemaphoreType.DMA((2,)),

time: 32.7 us -> 32.6 us (level)
  no operation moved by 1% of the time
where the time goes in v8:
time: 32.6 us; the launch traced here: 32.4 us
  Pallas kernels  31.8 us (98%)
  between operations  0.64 us (2%)
    pallas_call x1, Pallas kernels, shards(): pl.pallas_call(kernel, out_shape=(out, out), in_specs=[pl.BlockSpec(memor...  31.1 us
    pallas_call x1, Pallas kernels, shards(): pl.pallas_call(write_out, out_shape=(out, out), in_specs=[pl.BlockSpec(me...  0.69 us

profile of v8, /device:TPU:47, one launch (start us, length us, event | category | flops | bytes accessed | tf_op | source)
XLA Modules:
  0.0 32.4 jit_solution(14022084576441301746)
XLA Ops:
  0.6 31.1 %pressure_step.1 = (f32[24,8,128]{2,1,0:T(8,128)S(1)}, f32[24,8,128]{2,1,0:T(8,128)S(1)}) custom-call(f32[24,8,128]{2,1,0:T(8,128)} %refs_0_.1, f32[3,24,8,128]{3,2,1,0:T(8,128)} %refs_1_.1, f32[3,24,8,128]{3,2,1,0:T(8,128)} %refs_2_.1, f32[10,3,10]{2,1,0:T(4,128)} %bitcast.4, f32[10,1,10]{2,1,0:T(1,128)} %bitcast.5, f32[10,16,10]{2,1,0:T(8,128)} %bitcast.3, ...), custom_call_target="tpu_custom_call" | custom-call | tf_op jit(solution)/shard_map/pressure_step/pallas_call | solution.py:602
  31.8 0.7 %write_out.1 = (f32[24,8,128]{2,1,0:T(8,128)}, f32[24,8,128]{2,1,0:T(8,128)}) custom-call(f32[24,8,128]{2,1,0:T(8,128)S(1)} %get-tuple-element.4.op_in, f32[24,8,128]{2,1,0:T(8,128)S(1)} %get-tuple-element.5.pre_in), custom_call_target="tpu_custom_call" | custom-call | tf_op jit(solution)/shard_map/write_out/pallas_call | solution.py:635

commit v9 on v4

--- a/solution.py
+++ b/solution.py
@@ -23,7 +23,7 @@
 F32 = jnp.float32
 BF16 = jnp.bfloat16
 MESH = pl.DeviceIdType.MESH
-N_IN = 17
+N_IN = 11
 RUN = 8
 BEHIND = (1, 5, 7)
 RELAY_LEN = 80
@@ -134,7 +134,12 @@
         if second_layer[col] >= 0:
             cols_second[LAYER_NODE[second_layer[col]] * 8 + 3, col] = 1.0
     exact = [t.astype(BF16) for t in (gather, pick, cols_first, cols_second)]
-    return [left_all, left_t] + thirds + exact
+    left_all = np.concatenate([left_all, np.zeros((128, 64), BF16)], axis=1)
+    near = np.concatenate([left_all, left_t] + thirds, axis=0)
+    gather, pick, cols_first, cols_second = exact
+    gather = np.concatenate([gather, np.zeros((128, 96), BF16)], axis=1)
+    wide = [t[:, k : k + 128] for t in (gather, cols_first, cols_second) for k in range(0, t.shape[1], 128)]
+    return [near, np.concatenate([pick] + wide, axis=0)]
 
 
 def dot(a, b):
@@ -147,7 +152,15 @@
 
 
 def product(a, b):
-    return dot(a[0], b[0]) + (dot(a[1], b[0]) + dot(a[0], b[1]))
+    rows = a[0].shape[0]
+    half = rows // 32 * 16 or rows
+    parts = []
+    for begin, end in ((0, half), (half, rows)):
+        if begin < end:
+            high, low = a[0][begin:end], a[1][begin:end]
+            both = dot(jnp.concatenate([high, low], axis=0), b[0])
+            parts.append(both[: end - begin] + (both[end - begin :] + dot(high, b[1])))
+    return jnp.concatenate(parts, axis=0)
 
 
 def lane_product(a, table):
@@ -159,11 +172,14 @@
     return dot(jnp.concatenate(a, axis=1), jnp.concatenate([b[0], b[0]], axis=0)) + dot(a[0], b[1])
 
 
+def dot_nt(a, b):
+    return lax.dot_general(a, b, (((1,), (1,)), ((), ())), preferred_element_type=F32)
+
+
 def product_nt(a, b):
-    def one(x, y):
-        return lax.dot_general(x, y, (((1,), (1,)), ((), ())), preferred_element_type=F32)
-
-    return one(a[0], b[0]) + (one(a[1], b[0]) + one(a[0], b[1]))
+    rows = a[0].shape[0]
+    both = dot_nt(jnp.concatenate(a, axis=0), b[0])
+    return both[:rows] + (both[rows:] + dot_nt(a[0], b[1]))
 
 
 def iota(shape, dimension):
@@ -209,15 +225,17 @@
         eigen_first,
         eigen_second,
         eigen_third,
-        left,
-        left_t,
-        third,
-        third_t,
-        gather,
-        pick,
-        cols_first,
-        cols_second,
+        near,
+        far,
     ) = vmem
+    left, left_t = near.at[0:128, 0:192], near.at[128:192, :]
+    third, third_t = near.at[192:448, :], near.at[448:704, :]
+    pick = far.at[0:ROWS, :]
+
+    def table(first, count):
+        parts = [far[ROWS + 128 * k : ROWS + 128 * (k + 1), :] for k in range(first, first + count)]
+        return jnp.concatenate(parts, axis=1)
+
     n_s, n_c = lax.axis_size("stream"), lax.axis_size("cross")
     me_s, me_c = lax.axis_index("stream"), lax.axis_index("cross")
 
@@ -278,7 +296,7 @@
     loads = [
         pltpu.make_async_copy(hbm[i], vmem[i], load_sem.at[i]) for i in range(N_IN)
     ]
-    order = [0, 9, 11, 1, 2, 10, 12, 5, 13, 3, 4, 14, 15, 16, 6, 7, 8]
+    order = [0, 9, 1, 2, 5, 3, 4, 10, 6, 7, 8]
     for i in order:
         loads[i].start()
 
@@ -286,7 +304,7 @@
     modes12[...] = jnp.zeros_like(modes12)
     eigen[...] = jnp.zeros_like(eigen)
 
-    for i in (0, 9, 11):
+    for i in (0, 9):
         loads[i].wait()
     pres = split(pressure[...].reshape(OWN, 128))
     per = N1 * N1
@@ -295,7 +313,7 @@
         high, low = (part[a * per : (a + 1) * per] for part in pres)
         along.append(dot(left[...], jnp.concatenate([high, low, high], axis=0)))
     grad_third = lane_product(pres, third[...])
-    for i in (1, 2, 10, 12):
+    for i in (1, 2):
         loads[i].wait()
     for a in range(AB):
         rows = pl.ds(a * N1, N1)
@@ -364,7 +382,7 @@
         pl.when(here)(sends[slot].start)
     to_relay(lambda slot: relayed[slot].start())
 
-    for i in order[7:]:
+    for i in order[4:]:
         loads[i].wait()
     for m in range(M):
         modes3[m * 16 : m * 16 + CB, 0:M] = modes_third[m]
@@ -385,7 +403,7 @@
     )
     for part in split(modes3[...]):
         diagonal = jnp.where(same, dot(part, spread), 0.0).astype(BF16)
-        moved = dot(gather[...], diagonal)
+        moved = dot(table(0, 2)[:, : CB * M], diagonal)
         fore.append(moved.astype(BF16))
         back.append(jnp.where(stays, moved, 0.0).astype(BF16))
 
@@ -396,8 +414,8 @@
     at_block = block_of(iota((ROWS, WIDE), 0)) == (iota((ROWS, WIDE), 1) & 7)
     by_p = jnp.where(at_block, picked, 0.0).astype(BF16)
     by_q = picked.astype(BF16)
-    forward = dot(by_p, jnp.concatenate([cols_first[...]] * 2, axis=0)) * dot(
-        by_q, jnp.concatenate([cols_second[...]] * 2, axis=0)
+    forward = dot(by_p, jnp.concatenate([table(2, 3)] * 2, axis=0)) * dot(
+        by_q, jnp.concatenate([table(5, 3)] * 2, axis=0)
     )
     own_split = split(forward[:, :OWN])
     halo_split = split(forward[:, OWN:])

time: 31.8 us -> 31.4 us (0.987)
  Pallas kernels: 31 us -> 30.6 us
    pallas_call x1, Pallas kernels: 30.3 us -> 29.9 us  [shards(): pl.pallas_call(kernel, out_shape=(out, out), in_specs=[pl.BlockSpec(memor...]
where the time goes in v9:
time: 31.4 us; the launch traced here: 31.2 us
  Pallas kernels  30.6 us (97%)
  between operations  0.64 us (2%)
    pallas_call x1, Pallas kernels, shards(): pl.pallas_call(kernel, out_shape=(out, out), in_specs=[pl.BlockSpec(memor...  29.9 us
    pallas_call x1, Pallas kernels, shards(): pl.pallas_call(write_out, out_shape=(out, out), in_specs=[pl.BlockSpec(me...  0.69 us

profile of v9, /device:TPU:47, one launch (start us, length us, event | category | flops | bytes accessed | tf_op | source)
XLA Modules:
  0.0 31.2 jit_solution(13325624865989915316)
XLA Ops:
  0.6 29.9 %pressure_step.1 = (f32[24,8,128]{2,1,0:T(8,128)S(1)}, f32[24,8,128]{2,1,0:T(8,128)S(1)}) custom-call(f32[24,8,128]{2,1,0:T(8,128)} %refs_0_.1, f32[3,24,8,128]{3,2,1,0:T(8,128)} %refs_1_.1, f32[3,24,8,128]{3,2,1,0:T(8,128)} %refs_2_.1, f32[10,3,10]{2,1,0:T(4,128)} %bitcast.4, f32[10,1,10]{2,1,0:T(1,128)} %bitcast.5, f32[10,16,10]{2,1,0:T(8,128)} %bitcast.3, ...), custom_call_target="tpu_custom_call" | custom-call | tf_op jit(solution)/shard_map/pressure_step/pallas_call | solution.py:560
  30.5 0.7 %write_out.1 = (f32[24,8,128]{2,1,0:T(8,128)}, f32[24,8,128]{2,1,0:T(8,128)}) custom-call(f32[24,8,128]{2,1,0:T(8,128)S(1)} %get-tuple-element.4.op_in, f32[24,8,128]{2,1,0:T(8,128)S(1)} %get-tuple-element.5.pre_in), custom_call_target="tpu_custom_call" | custom-call | tf_op jit(solution)/shard_map/write_out/pallas_call | solution.py:592

commit v10 on v9

--- a/solution.py
+++ b/solution.py
@@ -178,8 +178,13 @@
 
 def product_nt(a, b):
     rows = a[0].shape[0]
-    both = dot_nt(jnp.concatenate(a, axis=0), b[0])
-    return both[:rows] + (both[rows:] + dot_nt(a[0], b[1]))
+    half = rows // 32 * 16
+    parts = []
+    for begin, end in ((0, half), (half, rows)):
+        high, low = a[0][begin:end], a[1][begin:end]
+        both = dot_nt(jnp.concatenate([high, low], axis=0), b[0])
+        parts.append(both[: end - begin] + (both[end - begin :] + dot_nt(high, b[1])))
+    return jnp.concatenate(parts, axis=0)
 
 
 def iota(shape, dimension):
@@ -284,7 +289,7 @@
         pl.semaphore_signal(barrier, inc=1, device_id=peer(side_s, side_c), device_id_type=MESH)
 
     pl.when(is_last)(functools.partial(greet, 0, 2 - RUN))
-    for side_s, side_c in SLOTS:
+    for side_s, side_c in SLOTS[4:] + SLOTS[:4]:
         here = there(side_s, side_c)
         if side_c > 0:
             here = jnp.logical_and(here, jnp.logical_not(is_last))

time: 31.4 us -> 31.3 us (level)
  no operation moved by 1% of the time
where the time goes in v10:
time: 31.3 us; the launch traced here: 31.2 us
  Pallas kernels  30.5 us (97%)
  between operations  0.64 us (2%)
    pallas_call x1, Pallas kernels, shards(): pl.pallas_call(kernel, out_shape=(out, out), in_specs=[pl.BlockSpec(memor...  29.8 us
    pallas_call x1, Pallas kernels, shards(): pl.pallas_call(write_out, out_shape=(out, out), in_specs=[pl.BlockSpec(me...  0.69 us

profile of v10, /device:TPU:47, one launch (start us, length us, event | category | flops | bytes accessed | tf_op | source)
XLA Modules:
  0.0 31.2 jit_solution(15862061935197499900)
XLA Ops:
  0.6 29.8 %pressure_step.1 = (f32[24,8,128]{2,1,0:T(8,128)S(1)}, f32[24,8,128]{2,1,0:T(8,128)S(1)}) custom-call(f32[24,8,128]{2,1,0:T(8,128)} %refs_0_.1, f32[3,24,8,128]{3,2,1,0:T(8,128)} %refs_1_.1, f32[3,24,8,128]{3,2,1,0:T(8,128)} %refs_2_.1, f32[10,3,10]{2,1,0:T(4,128)} %bitcast.4, f32[10,1,10]{2,1,0:T(1,128)} %bitcast.5, f32[10,16,10]{2,1,0:T(8,128)} %bitcast.3, ...), custom_call_target="tpu_custom_call" | custom-call | tf_op jit(solution)/shard_map/pressure_step/pallas_call | solution.py:565
  30.5 0.7 %write_out.1 = (f32[24,8,128]{2,1,0:T(8,128)}, f32[24,8,128]{2,1,0:T(8,128)}) custom-call(f32[24,8,128]{2,1,0:T(8,128)S(1)} %get-tuple-element.4.op_in, f32[24,8,128]{2,1,0:T(8,128)S(1)} %get-tuple-element.5.pre_in), custom_call_target="tpu_custom_call" | custom-call | tf_op jit(solution)/shard_map/write_out/pallas_call | solution.py:597
